TPU v7x, 32 devices: a whole 2x2x4 slice. The times are simulated.
32 devices in a mesh: hist: 8 (over z, y), second: 4 (over x, core).
Axes of the slice: x: 2, y: 2, z: 4, core: 2. Of those that a mesh axis runs over, the one named last changes fastest.
Arguments:
- history: bfloat16 [32, 64, 32, 2, 128], P('hist', None, 'second'), may hold values from -0.29882812 to 0.29882812
- row_now: float32 [64, 32, 256], P('hist', 'second'), may hold values from -4.2 to 4.2
- coupling: float32 [64, 64], P('hist'), may hold values from 0.5 to 1.5
- step_inverse: float32 [3, 2, 64, 64], replicated, may hold values from -0.5 to 0.5
- start_step: int32 [1], replicated, may hold values from 16 to 28
- history_time: int32 [32], P('hist'), may hold values from 0 to 31, each once
Outputs:
- green_next: float32 [64, 32, 256], P('hist', 'second')
Inputs may be any that keep to these rules, and one draw needn't show every extreme that they name: history_time holds every time from 0 to 31 once.
All inputs are finite; a program needn't handle non-finite values.
Results may differ from a plain program's by a relative error of at most 0.011.
Values may be sent and summed in bfloat16 or wider, within the bound.
No kernel may reach another device: no remote copies, remote signals or barrier semaphores. Data moves between devices by JAX's collectives and lax.ppermute only.
A program may use at most 64 MiB of HBM per device.

v0:
```python
import jax
import jax.numpy as jnp
from jax import lax
from jax.sharding import PartitionSpec as P

step_width = 0.05
highest = lax.Precision.HIGHEST


def cubic_term(first_real, first_imag, other_real, other_imag):
    square_real = first_real * first_real - first_imag * first_imag
    square_imag = 2.0 * first_real * first_imag
    return (
        square_real * other_real + square_imag * other_imag,
        square_imag * other_real - square_real * other_imag,
    )


def self_energy(green_row, coupling):
    weight_sq = (coupling * coupling)[:, None, :]
    lesser_real, lesser_imag = (green_row[:, :, 0, 0], green_row[:, :, 0, 1])
    greater_real, greater_imag = (green_row[:, :, 1, 0], green_row[:, :, 1, 1])
    less_real, less_imag = cubic_term(lesser_real, lesser_imag, greater_real, greater_imag)
    more_real, more_imag = cubic_term(greater_real, greater_imag, lesser_real, lesser_imag)
    diff_real = weight_sq * (more_real - less_real)
    diff_imag = weight_sq * (more_imag - less_imag)
    stacked = jnp.stack([diff_real, diff_imag], axis=2)
    return stacked.reshape(green_row.shape[0], green_row.shape[1], 2 * green_row.shape[4]).astype(
        jnp.bfloat16
    )


def advance(green_row, summed, inverse_pair):
    real_sum = summed[:, :, :, 0, 0, :] - summed[:, :, :, 1, 1, :]
    imag_sum = summed[:, :, :, 1, 0, :] + summed[:, :, :, 0, 1, :]
    moved_real = green_row[:, :, :, 0, :] + step_width * real_sum
    moved_imag = green_row[:, :, :, 1, :] + step_width * imag_sum
    inverse_real = inverse_pair[0]
    inverse_imag = inverse_pair[1]
    new_real = jnp.einsum(
        "xa,btma->btmx", inverse_real, moved_real, precision=highest
    ) - jnp.einsum("xa,btma->btmx", inverse_imag, moved_imag, precision=highest)
    new_imag = jnp.einsum(
        "xa,btma->btmx", inverse_real, moved_imag, precision=highest
    ) + jnp.einsum("xa,btma->btmx", inverse_imag, moved_real, precision=highest)
    return jnp.stack([new_real, new_imag], axis=3)


def contract(selected, history_block):
    return jnp.einsum(
        "jsqa,sjtmbp->btmpqa", selected, history_block, preferred_element_type=jnp.float32
    )


def body(history, row_now, coupling, step_inverse, start_step, history_time):
    orbitals = history.shape[1]
    own_rows = row_now.shape[0]
    slab = row_now.shape[1]
    anchor = start_step[0]
    local_history = lax.all_to_all(history, "hist", split_axis=4, concat_axis=0, tiled=True)
    local_times = lax.all_gather(history_time, "hist", axis=0, tiled=True)
    slots = local_history.shape[0]
    alive_slot = local_times <= anchor
    green_row = row_now.reshape(own_rows, slab, 2, 2, orbitals)
    earlier = []
    for window_step in range(step_inverse.shape[0]):
        energy = self_energy(green_row, coupling)
        by_orbital = lax.all_gather(energy, "hist", axis=0, tiled=True)
        whole_row = lax.all_gather(by_orbital, "second", axis=1, tiled=True)
        energy_left = whole_row.reshape(orbitals, whole_row.shape[1], 2, orbitals)
        selected = jnp.take(energy_left, local_times, axis=1)
        selected = jnp.where(alive_slot[None, :, None, None], selected, jnp.zeros((), jnp.bfloat16))
        history_block = local_history.reshape(slots, orbitals, slab, 2, own_rows, 2)
        summed = contract(selected, history_block)
        for past_index, past_row in enumerate(earlier):
            column = lax.dynamic_index_in_dim(
                energy_left, anchor + 1 + past_index, 1, keepdims=False
            ).astype(jnp.float32)
            summed = summed + jnp.einsum("jqa,btmpj->btmpqa", column, past_row, precision=highest)
        green_row = advance(green_row, summed, step_inverse[window_step])
        earlier.append(green_row)
    return green_row.reshape(own_rows, slab, 4 * orbitals)


def solution(mesh):
    placed = (
        P("hist", None, "second", None, None),
        P("hist", "second", None),
        P("hist", None),
        P(),
        P(),
        P("hist"),
    )
    return jax.shard_map(
        body, mesh=mesh, in_specs=placed, out_specs=P("hist", "second", None), check_vma=False
    )
```

profile of v0, /device:TPU:0, one launch (start us, length us, event | category | flops | bytes accessed | tf_op | source)
XLA Modules:
  0.0 179.3 jit_solution(12316832551157023155)
XLA Ops:
  0.0 5.2 %copy.167 = bf16[4,64,8,2,128]{1,3,2,0,4:T(2,128)(2,1)S(1)} copy(bf16[4,64,8,2,128]{4,3,2,1,0:T(2,128)(2,1)} %param.8) | data formatting | bytes 2097152 | tf_op args[0]
  5.3 2.7 %reshape.795 = bf16[8,2,32768]{2,1,0:T(2,128)(2,1)} reshape(bf16[128,4,8,2,64]{4,3,2,1,0:T(2,128)(2,1)S(1)} %bitcast.277) | data formatting | bytes 2097152
  7.9 7.3 %all-to-all-start = ((bf16[8,2,32768]{2,1,0:T(2,128)(2,1)}), bf16[8,2,32768]{2,1,0:T(2,128)(2,1)S(1)}, u32[]{:S(2)}, u32[]{:S(2)}) async-start(bf16[8,2,32768]{2,1,0:T(2,128)(2,1)} %reshape.795), calls=%async_computation | async-start | bytes 2097152 | tf_op jit(solution)/shard_map/all_to_all | solution.py:60
  16.4 44.8 %all_gather.22 = bf16[64,8,128]{2,1,0:T(8,128)(2,1)S(1)} all-gather(bf16[8,8,128]{2,1,0:T(8,128)(2,1)S(1)} %convert_element_type.15), channel_id=1, replica_groups=mesh['hist'=8,'second'=4] {'hist'}, dimensions={0}, use_global_device_ids=true | all-gather | bytes 147456 | tf_op jit(solution)/shard_map/all_gather | solution.py:68
  61.1 7.3 %all_gather.23 = bf16[64,32,128]{2,1,0:T(8,128)(2,1)S(1)} all-gather(bf16[64,8,128]{2,1,0:T(8,128)(2,1)S(1)} %all_gather.22), channel_id=1, replica_groups=mesh['hist'=8,'second'=4] {'second'}, dimensions={1}, use_global_device_ids=true | all-gather | bytes 655360 | tf_op jit(solution)/shard_map/all_gather | solution.py:69
  68.8 1.2 copy.166
  70.1 0.6 dynamic-slice
  71.6 8.9 %all-reduce = s32[32]{0:T(128)S(1)} all-reduce(s32[32]{0:T(128)S(1)} %dynamic-update-slice), channel_id=1, replica_groups=mesh['hist'=8,'second'=4] {'hist'}, use_global_device_ids=true, to_apply=%add | all-reduce | flops 32 | bytes 256
  80.6 1.6 gather_fusion
  82.3 1.4 reshape.796
  83.8 2.4 %copy.168 = bf16[4,64,8,2,128]{1,4,3,2,0:T(8,128)(2,1)S(1)} copy(bf16[4,64,8,2,128]{1,3,2,0,4:T(2,128)(2,1)S(1)} %bitcast.278) | data formatting | bytes 2097152 | tf_op jit(solution)/shard_map/all_to_all | solution.py:60
  86.2 2.4 %copy.169 = bf16[8,4,64,8,2,16]{2,3,5,4,1,0:T(8,128)(2,1)S(1)} copy(bf16[8,4,64,8,2,16]{2,5,0,4,3,1:T(8,128)(2,1)S(1)} %bitcast.279) | data formatting | bytes 2097152 | tf_op jit(solution)/shard_map/all_to_all | solution.py:60
  88.7 0.9 fusion.7
  91.1 30.5 %all_gather.24 = bf16[64,8,128]{2,1,0:T(8,128)(2,1)S(1)} all-gather(bf16[8,8,128]{2,1,0:T(8,128)(2,1)S(1)} %convert_element_type.16), channel_id=1, replica_groups=mesh['hist'=8,'second'=4] {'hist'}, dimensions={0}, use_global_device_ids=true | all-gather | bytes 147456 | tf_op jit(solution)/shard_map/all_gather | solution.py:68
  121.7 6.7 %all_gather.25 = bf16[64,32,128]{2,1,0:T(8,128)(2,1)S(1)} all-gather(bf16[64,8,128]{2,1,0:T(8,128)(2,1)S(1)} %all_gather.24), channel_id=1, replica_groups=mesh['hist'=8,'second'=4] {'second'}, dimensions={1}, use_global_device_ids=true | all-gather | bytes 655360 | tf_op jit(solution)/shard_map/all_gather | solution.py:69
  128.8 1.2 copy.182
  130.1 0.7 gather_fusion.1
  130.8 2.4 %fusion.10 = f32[8,8,2,2,2,64]{5,0,1,2,4,3:T(8,128)S(1)} fusion(bf16[32,64,8,2,8,2,1]{1,2,5,4,3,0,6:T(8,128)(2,1)} %bitcast.281, bf16[32,64,2,64]{3,1,2,0:T(8,128)(2,1)S(1)} %gather_fusion.1, pred[32]{0:T(512)(128)(4,1)S(1)} %get-tuple-element.27, pred[32]{0:T(512)(128)(4,1)S(1)} %get-tuple-element.26), kind=kOutput, calls=%fused_computation.11 | convolution fusion | flops 134742016 | bytes 1704000 | tf_op jit(solution)/shard_map/jsqa,sjtmbp->btmpqa/dot_general | solution.py:50
  134.6 30.5 %all_gather.26 = bf16[64,8,128]{2,1,0:T(8,128)(2,1)S(1)} all-gather(bf16[8,8,128]{2,1,0:T(8,128)(2,1)S(1)} %convert_element_type.17), channel_id=1, replica_groups=mesh['hist'=8,'second'=4] {'hist'}, dimensions={0}, use_global_device_ids=true | all-gather | bytes 147456 | tf_op jit(solution)/shard_map/all_gather | solution.py:68
  165.1 6.9 %all_gather.27 = bf16[64,32,128]{2,1,0:T(8,128)(2,1)S(1)} all-gather(bf16[64,8,128]{2,1,0:T(8,128)(2,1)S(1)} %all_gather.26), channel_id=1, replica_groups=mesh['hist'=8,'second'=4] {'second'}, dimensions={1}, use_global_device_ids=true | all-gather | bytes 655360 | tf_op jit(solution)/shard_map/all_gather | solution.py:69
  172.4 1.2 copy.202
  173.8 0.7 gather_fusion.2
  174.5 2.4 %fusion.13 = f32[8,8,2,2,2,64]{5,0,2,1,4,3:T(8,128)S(1)} fusion(bf16[32,64,8,2,8,2,1]{1,2,5,4,3,0,6:T(8,128)(2,1)} %bitcast.282, bf16[32,64,2,64]{3,1,2,0:T(8,128)(2,1)S(1)} %gather_fusion.2, pred[32]{0:T(512)(128)(4,1)S(1)} %get-tuple-element.27, pred[32]{0:T(512)(128)(4,1)S(1)} %get-tuple-element.26), kind=kOutput, calls=%fused_computation.12 | convolution fusion | flops 134742016 | bytes 1704000 | tf_op jit(solution)/shard_map/jsqa,sjtmbp->btmpqa/dot_general | solution.py:50
  178.5 0.8 reshape.735
  (61 shorter events, 6.4 us)
Async XLA Ops:
  5.2 10.6 %copy-start.4 = (f32[8,64]{1,0:T(8,128)S(1)}, f32[8,64]{1,0:T(8,128)}, u32[]{:S(2)}) copy-start(f32[8,64]{1,0:T(8,128)} %param.10) | copy-start | bytes 6148
  5.2 10.7 %copy-start.3 = (f32[8,8,256]{2,1,0:T(8,128)S(1)}, f32[8,8,256]{2,1,0:T(8,128)}, u32[]{:S(2)}) copy-start(f32[8,8,256]{2,1,0:T(8,128)} %param.9) | copy-start | bytes 196612
  7.9 74.4 %all-to-all-start = ((bf16[8,2,32768]{2,1,0:T(2,128)(2,1)}), bf16[8,2,32768]{2,1,0:T(2,128)(2,1)S(1)}, u32[]{:S(2)}, u32[]{:S(2)}) async-start(bf16[8,2,32768]{2,1,0:T(2,128)(2,1)} %reshape.795), calls=%async_computation | async-start | bytes 2097152 | tf_op jit(solution)/shard_map/all_to_all | solution.py:60
  61.1 9.0 %copy-start.6 = (u32[32]{0:T(128)S(1)}, u32[32]{0:T(128)}, u32[]{:S(2)}) copy-start(u32[32]{0:T(128)} %constant.37) | copy-start | bytes 388
  61.1 10.2 %copy-start.5 = (s32[4]{0:T(128)S(1)}, s32[4]{0:T(128)}, u32[]{:S(2)}) copy-start(s32[4]{0:T(128)} %param.13) | copy-start | bytes 52
  86.2 2.5 %copy-start.1 = (bf16[32,64,2,64]{3,1,2,0:T(8,128)(2,1)S(1)}, bf16[32,64,2,64]{3,1,2,0:T(8,128)(2,1)}, u32[]{:S(2)}) copy-start(bf16[32,64,2,64]{3,1,2,0:T(8,128)(2,1)} %gather_fusion) | copy-start | bytes 1572868
  88.7 1.3 copy-start
  88.7 1.4 copy-start.2
where the time goes:
time: 180 us; the launch traced here: 179 us
  blocking collectives  136 us (76%)
  local copies, waits for them, and re-layouts  25.2 us (14%)
  matrix products  8.98 us (5%)
  starting transfers between devices  7.31 us (4%)
  between operations  1.8 us (1%)
    all_gather x3, blocking collectives, body(): by_orbital = lax.all_gather(energy, 'hist', axis=0, tiled=True)  106 us
    all_gather x3, blocking collectives, body(): whole_row = lax.all_gather(by_orbital, 'second', axis=1, tiled=True)  20.9 us
    unnamed x20, local copies, waits for them, and re-layouts  10.6 us
    unnamed x1, blocking collectives  8.94 us
    all_to_all x1, starting transfers between devices, body(): lax.all_to_all(history, 'hist', split_axis=4, concat_axis=0, tiled=True)  7.31 us
    dot_general x3, matrix products, contract(): jnp.einsum('jsqa,sjtmbp->btmpqa', selected, history_block, preferred_elem...  5.77 us
    all_to_all x2, local copies, waits for them, and re-layouts, body(): lax.all_to_all(history, 'hist', split_axis=4, concat_axis=0, tiled=True)  4.87 us
    reshape x6, local copies, waits for them, and re-layouts, body(): energy_left = whole_row.reshape(orbitals, whole_row.shape[1], 2, orbitals)  4.86 us
  transfers between devices with their start and end apart: 1, of which 0 were waited for; matrix products, arithmetic and copies ran while one was open for 3% of the time, Pallas kernels for 0%

commit v1 on v0

v1 whole, which is shorter than its diff:
```python
import functools

import jax
import jax.numpy as jnp
from jax import lax
from jax.experimental import pallas as pl
from jax.experimental.pallas import tpu as pltpu
from jax.sharding import Mesh, PartitionSpec as P

step_width = 0.05
highest = lax.Precision.HIGHEST
bf16 = jnp.bfloat16
f32 = jnp.float32
vmem = pl.BlockSpec(memory_space=pltpu.VMEM)
smem = pl.BlockSpec(memory_space=pltpu.SMEM)


def pack_kernel(groups, peers, hist_ref, out_ref, wide_ref):
    rows = hist_ref.shape[0] // groups
    width = hist_ref.shape[1] // peers
    wide_ref[...] = hist_ref[...].astype(f32)
    for group in range(groups):
        turned = wide_ref[pl.ds(group, rows, stride=groups), :].T.astype(bf16)
        for peer in range(peers):
            out_ref[peer, group * width : (group + 1) * width, :] = turned[
                peer * width : (peer + 1) * width
            ]


def cubic_term(first_real, first_imag, other_real, other_imag):
    square_real = first_real * first_real - first_imag * first_imag
    square_imag = 2.0 * first_real * first_imag
    return (
        square_real * other_real + square_imag * other_imag,
        square_imag * other_real - square_real * other_imag,
    )


def energy_of(lesser, greater, weight_sq):
    half = lesser.shape[-1] // 2
    lr, li = lesser[:, :half], lesser[:, half:]
    gr, gi = greater[:, :half], greater[:, half:]
    less_real, less_imag = cubic_term(lr, li, gr, gi)
    more_real, more_imag = cubic_term(gr, gi, lr, li)
    return jnp.concatenate(
        [weight_sq * (more_real - less_real), weight_sq * (more_imag - less_imag)], axis=-1
    )


def send_energy(row_ref, coupling_ref, scratch_ref, send_ref):
    own_rows, slab, lanes = row_ref.shape
    for b in range(own_rows):
        row = row_ref[b]
        weight = coupling_ref[b : b + 1, :]
        scratch_ref[pl.ds(b, slab, stride=own_rows), :] = energy_of(
            row[:, : lanes // 2], row[:, lanes // 2 :], weight * weight
        )
    narrow = scratch_ref[...].astype(bf16)
    for peer in range(send_ref.shape[0]):
        send_ref[peer, : own_rows * slab, :] = narrow


def first_kernel(row_ref, coupling_ref, time_ref, send_ref, scratch_ref):
    own_rows, slab, lanes = row_ref.shape
    send_energy(row_ref, coupling_ref, scratch_ref, send_ref)
    pad = send_ref.shape[1] - own_rows * slab
    lane = lax.broadcasted_iota(jnp.int32, (pad, lanes // 2), 1)
    times = jnp.zeros((pad, lanes // 2), jnp.int32)
    for slot in range(time_ref.shape[0]):
        times = jnp.where(lane == slot, time_ref[slot], times)
    times = times.astype(f32).astype(bf16)
    for peer in range(send_ref.shape[0]):
        send_ref[peer, own_rows * slab :, :] = times


def step_kernel(
    n_past, last, time_ref, anchor_ref, core_ref, hist_ref, own_ref, other_ref, row_ref, *rest
):
    past_refs = rest[:n_past]
    inverse_ref, coupling_ref, out_ref = rest[n_past : n_past + 3]
    rest = rest[n_past + 3 :]
    if last:
        chosen_ref, sum_ref = rest
        send_ref = energy_ref = None
    else:
        send_ref, chosen_ref, sum_ref, energy_ref = rest
    peers, slab, own_rows = own_ref.shape[0], own_ref.shape[2], own_ref.shape[3]
    orbitals = peers * own_rows
    lanes = own_ref.shape[4]
    half = lanes // 2
    slots = time_ref.shape[0]
    block = slots // peers
    anchor = anchor_ref[0]
    core = core_ref[0]

    def energy_at(time):
        inner = lax.rem(time, slab)
        group = lax.div(time, slab)
        far = lax.div(group, 2)
        same = lax.rem(group, 2) == core
        return [
            jnp.where(same, own_ref[peer, far, inner], other_ref[peer, far, inner])
            for peer in range(peers)
        ]

    def choose(slot, carry):
        time = time_ref[slot]
        alive = time <= anchor
        for peer, part in enumerate(energy_at(time)):
            chosen_ref[slot, peer * own_rows : (peer + 1) * own_rows, :] = jnp.where(
                alive, part, jnp.zeros_like(part)
            )
        return carry

    lax.fori_loop(0, slots, choose, 0, unroll=slots <= 32)
    total = None
    for peer in range(peers):
        part = jnp.dot(
            hist_ref[peer],
            chosen_ref[peer * block : (peer + 1) * block].reshape(block * orbitals, lanes),
            preferred_element_type=f32,
        )
        total = part if total is None else total + part
    sum_ref[...] = total
    sign = jnp.where(lax.broadcasted_iota(jnp.int32, (1, lanes), 1) < half, -1.0, 1.0)
    columns = []
    for past in range(n_past):
        for peer, part in enumerate(energy_at(anchor + 1 + past)):
            chosen_ref[past, peer * own_rows : (peer + 1) * own_rows, :] = part
        columns.append(chosen_ref[past])
    for m in range(2):
        evens, odds = [], []
        for b in range(own_rows):
            first = m * 2 * own_rows + 2 * b
            evens.append(sum_ref[pl.ds(first, slab, stride=4 * own_rows), :])
            odds.append(sum_ref[pl.ds(first + 1, slab, stride=4 * own_rows), :])
        even = jnp.concatenate(evens, axis=0)
        odd = jnp.concatenate(odds, axis=0)
        for past_ref, column in zip(past_refs, columns):
            for part in range(2):
                start = m * lanes + part * half
                row = past_ref[:, :, start : start + half].reshape(own_rows * slab, half)
                high = row.astype(bf16)
                low = (row - high.astype(f32)).astype(bf16)
                product = jnp.dot(high, column, preferred_element_type=f32) + jnp.dot(
                    low, column, preferred_element_type=f32
                )
                if part == 0:
                    even = even + product
                else:
                    odd = odd + product
        integral = even + sign * pltpu.roll(odd, half, 1)
        row = row_ref[:, :, m * lanes : (m + 1) * lanes].reshape(own_rows * slab, lanes)
        moved = row + step_width * integral
        moved = lax.dot_general(
            moved, inverse_ref[...], (((1,), (1,)), ((), ())), precision=highest,
            preferred_element_type=f32,
        )
        out_ref[:, :, m * lanes : (m + 1) * lanes] = moved.reshape(own_rows, slab, lanes)
    if not last:
        send_energy(out_ref, coupling_ref, energy_ref, send_ref)


def body(history, row_now, coupling, step_inverse, start_step, history_time):
    slots_dev, orbitals, slab, parts, lanes = history.shape
    own_rows = row_now.shape[0]
    steps = step_inverse.shape[0]
    peers = lax.axis_size("hist")
    far = lax.axis_size("x")
    groups = slab * parts
    width = lanes // peers
    n_sum = groups * width
    shape = jax.ShapeDtypeStruct
    packed = pl.pallas_call(
        functools.partial(pack_kernel, groups, peers),
        out_shape=shape((peers, n_sum, slots_dev * orbitals), bf16),
        in_specs=[vmem],
        out_specs=vmem,
        scratch_shapes=[pltpu.VMEM((slots_dev * orbitals * groups, lanes), f32)],
        name="pack",
    )(history.reshape(slots_dev * orbitals * groups, lanes))
    local = lax.all_to_all(packed, "hist", split_axis=0, concat_axis=0, tiled=True)
    pad = 16
    rows = slab * own_rows
    sent = pl.pallas_call(
        first_kernel,
        out_shape=shape((peers * far, rows + pad, lanes), bf16),
        in_specs=[vmem, vmem, smem],
        out_specs=vmem,
        scratch_shapes=[pltpu.VMEM((rows, lanes), f32)],
        name="first",
    )(row_now, coupling, history_time)
    real, imag = step_inverse[:, 0], step_inverse[:, 1]
    inverse = jnp.concatenate(
        [jnp.concatenate([real, -imag], axis=2), jnp.concatenate([imag, real], axis=2)], axis=1
    )
    core = lax.axis_index("c").reshape(1)
    green, past = row_now, []
    times = None
    for w in range(steps):
        last = w == steps - 1
        own = lax.all_to_all(sent, ("hist", "x"), split_axis=0, concat_axis=0, tiled=True)
        if w == 0:
            times = own.reshape(peers, far, rows + pad, lanes)[:, 0, rows, :slots_dev]
            times = times.astype(jnp.int32).reshape(peers * slots_dev)
            own = own[:, :rows]
        other = lax.ppermute(own, "c", [(0, 1), (1, 0)])
        split = (peers, far, slab, own_rows, lanes)
        outs = [shape(row_now.shape, f32)]
        scratch = [
            pltpu.VMEM((peers * slots_dev, orbitals, lanes), bf16),
            pltpu.VMEM((n_sum, lanes), f32),
        ]
        if not last:
            outs.append(shape((peers * far, rows, lanes), bf16))
            scratch.append(pltpu.VMEM((rows, lanes), f32))
        result = pl.pallas_call(
            functools.partial(step_kernel, len(past), last),
            out_shape=outs,
            in_specs=[smem] * 3 + [vmem] * (6 + len(past)),
            out_specs=[vmem] * len(outs),
            scratch_shapes=scratch,
            name=f"step{w}",
        )(
            times,
            start_step,
            core,
            local,
            own.reshape(split),
            other.reshape(split),
            green,
            *past,
            inverse[w],
            coupling,
        )
        green = result[0]
        if not last:
            sent = result[1]
            past.append(green)
    return green


def solution(mesh):
    n_hist, n_second = mesh.devices.shape
    split = Mesh(mesh.devices.reshape(n_hist, n_second // 2, 2), ("hist", "x", "c"))
    second = ("x", "c")
    placed = (
        P("hist", None, second, None, None),
        P("hist", second, None),
        P("hist", None),
        P(),
        P(),
        P("hist"),
    )
    return jax.shard_map(
        body, mesh=split, in_specs=placed, out_specs=P("hist", second, None), check_vma=False
    )
```

time: 180 us -> 93.5 us (0.52)
  blocking collectives: 136 us -> 27.4 us
  waiting for transfers between devices: 0.01 us -> 34.4 us
  local copies, waits for them, and re-layouts: 25.2 us -> 3.77 us
  Pallas kernels: 0 us -> 14.5 us
  matrix products: 8.98 us -> 0 us
  starting transfers between devices: 7.31 us -> 12 us
    all_gather x6 -> x0, blocking collectives: 127 us -> none  [the longest x3 106 us: body(): by_orbital = lax.all_gather(energy, 'hist', axis=0, tiled=True)]
    all_to_all x1 -> x2, waiting for transfers between devices: 0.01 us -> 31.3 us  [the longest x1 22.9 us: body(): lax.all_to_all(packed, 'hist', split_axis=0, concat_axis=0, tiled=True)]
    all_to_all x0 -> x2, blocking collectives: none -> 27.4 us  [body(): lax.all_to_all(sent, ('hist', 'x'), split_axis=0, concat_axis=0, tiled=True)]
    pallas_call x0 -> x5, Pallas kernels: none -> 14.5 us  [the longest x3 9.75 us: body(): pl.pallas_call(functools.partial(step_kernel, len(past), last), out_shape...]
    dot_general x18 -> x0, matrix products: 8.98 us -> none  [the longest x3 5.77 us: contract(): jnp.einsum('jsqa,sjtmbp->btmpqa', selected, history_block, preferred_elem...]
    unnamed x1 -> x0, blocking collectives: 8.94 us -> none
    unnamed x20 -> x16, local copies, waits for them, and re-layouts: 10.6 us -> 2.39 us
    reshape x8 -> x0, local copies, waits for them, and re-layouts: 5.77 us -> none  [the longest x6 4.86 us: body(): energy_left = whole_row.reshape(orbitals, whole_row.shape[1], 2, orbitals)]
  transfers between devices with their start and end apart: 1 -> 5, of which waited for: 0 -> 4; matrix products, arithmetic and copies ran while one was open for 3% -> 2% of each run, Pallas kernels for 0% -> 3%
where the time goes in v1:
time: 93.5 us; the launch traced here: 92.9 us
  waiting for transfers between devices  34.4 us (37%)
  blocking collectives  27.4 us (29%)
  Pallas kernels  14.5 us (16%)
  starting transfers between devices  12 us (13%)
  local copies, waits for them, and re-layouts  3.77 us (4%)
    all_to_all x2, blocking collectives, body(): lax.all_to_all(sent, ('hist', 'x'), split_axis=0, concat_axis=0, tiled=True)  27.4 us
    all_to_all x1, waiting for transfers between devices, body(): lax.all_to_all(packed, 'hist', split_axis=0, concat_axis=0, tiled=True)  22.9 us
    pallas_call x3, Pallas kernels, body(): pl.pallas_call(functools.partial(step_kernel, len(past), last), out_shape...  9.75 us
    all_to_all x1, waiting for transfers between devices, body(): lax.all_to_all(sent, ('hist', 'x'), split_axis=0, concat_axis=0, tiled=True)  8.35 us
    all_to_all x1, starting transfers between devices, body(): lax.all_to_all(sent, ('hist', 'x'), split_axis=0, concat_axis=0, tiled=True)  8.34 us
    all_to_all x1, starting transfers between devices, body(): lax.all_to_all(packed, 'hist', split_axis=0, concat_axis=0, tiled=True)  3.56 us
    ppermute x3, waiting for transfers between devices, body(): other = lax.ppermute(own, 'c', [(0, 1), (1, 0)])  3.07 us
    pallas_call x1, Pallas kernels, body(): pl.pallas_call(functools.partial(pack_kernel, groups, peers), out_shape=s...  2.97 us
  transfers between devices with their start and end apart: 5, of which 4 were waited for; matrix products, arithmetic and copies ran while one was open for 2% of the time, Pallas kernels for 3%

profile of v1, /device:TPU:0, one launch (start us, length us, event | category | flops | bytes accessed | tf_op | source)
XLA Modules:
  0.0 92.9 jit_solution(2271882751964247357)
XLA Ops:
  0.0 1.8 %first.1 = bf16[16,80,128]{2,1,0:T(8,128)(2,1)} custom-call(f32[8,8,256]{2,1,0:T(8,128)} %row_ref.3, f32[8,64]{1,0:T(8,128)} %rest_3_.1, s32[4]{0:T(128)} %time_ref.1), custom_call_target="tpu_custom_call" | custom-call | tf_op jit(solution)/shard_map/first/pallas_call | solution.py:185
  1.8 8.3 %all-to-all-start = ((bf16[16,80,128]{2,1,0:T(8,128)(2,1)}), bf16[16,80,128]{2,1,0:T(8,128)(2,1)S(1)}, u32[]{:S(2)}, u32[]{:S(2)}) async-start(bf16[16,80,128]{2,1,0:T(8,128)(2,1)} %first.1), calls=%async_computation | async-start | bytes 655360 | tf_op jit(solution)/shard_map/all_to_all | solution.py:202
  10.1 3.0 %pack.1 = bf16[8,256,256]{2,1,0:T(8,128)(2,1)} custom-call(bf16[4096,128]{1,0:T(8,128)(2,1)} %bitcast.31), custom_call_target="tpu_custom_call" | custom-call | tf_op jit(solution)/shard_map/pack/pallas_call | solution.py:174
  13.1 8.3 %all-to-all-done = bf16[16,80,128]{2,1,0:T(8,128)(2,1)S(1)} async-done(((bf16[16,80,128]{2,1,0:T(8,128)(2,1)}), bf16[16,80,128]{2,1,0:T(8,128)(2,1)S(1)}, u32[]{:S(2)}, u32[]{:S(2)}) %all-to-all-start) | async-done | bytes 327712 | tf_op jit(solution)/shard_map/all_to_all | solution.py:202
  21.4 3.6 %all-to-all-start.1 = ((bf16[8,256,256]{2,1,0:T(8,128)(2,1)}), bf16[8,256,256]{2,1,0:T(8,128)(2,1)S(1)}, u32[]{:S(2)}, u32[]{:S(2)}) async-start(bf16[8,256,256]{2,1,0:T(8,128)(2,1)} %pack.1), calls=%async_computation.1 | async-start | bytes 2097152 | tf_op jit(solution)/shard_map/all_to_all | solution.py:182
  25.1 0.1 maximum_maximum_fusion
  25.2 0.1 collective-permute-start
  25.3 0.7 slice_bitcast_fusion.2
  26.7 0.6 reshape.40.time_ref
  27.3 0.0 collective-permute-done
  27.3 22.9 %all-to-all-done.1.hist_ref = bf16[8,256,256]{2,1,0:T(8,128)(2,1)S(1)} async-done(((bf16[8,256,256]{2,1,0:T(8,128)(2,1)}), bf16[8,256,256]{2,1,0:T(8,128)(2,1)S(1)}, u32[]{:S(2)}, u32[]{:S(2)}) %all-to-all-start.1) | async-done | bytes 1048608 | tf_op jit(solution)/shard_map/all_to_all | solution.py:182
  50.3 1.0 %copy-done = bf16[8,256,256]{2,1,0:T(8,128)(2,1)} copy-done((bf16[8,256,256]{2,1,0:T(8,128)(2,1)}, bf16[8,256,256]{2,1,0:T(8,128)(2,1)S(1)}, u32[]{:S(2)}) %copy-start) | copy-done | bytes 1048600
  51.3 3.3 %step0.1 = (f32[8,8,256]{2,1,0:T(8,128)}, bf16[16,64,128]{2,1,0:T(8,128)(2,1)}) custom-call(s32[32]{0:T(128)} %reshape.40.time_ref, s32[1]{0:T(128)S(6)} %copy.17.anchor_ref, s32[1]{0:T(128)} %bitcast.1.core_ref, bf16[8,256,256]{2,1,0:T(8,128)(2,1)} %copy-done, bf16[8,2,8,8,128]{4,3,2,1,0:T(8,128)(2,1)} %bitcast.32, bf16[8,2,8,8,128]{4,3,2,1,0:T(8,128)(2,1)} %bitcast.35, ...), custom_call_target="tpu_custom_call" | custom-call | tf_op jit(solution)/shard_map/step0/pallas_call | solution.py:217
  54.6 13.5 %all_to_all.20 = bf16[16,64,128]{2,1,0:T(8,128)(2,1)S(1)} all-to-all(bf16[16,64,128]{2,1,0:T(8,128)(2,1)} %get-tuple-element.9), channel_id=1, replica_groups=mesh['hist'=8,'x'=2,'c'=2] {'hist','x'}, dimensions={0} | all-to-all | bytes 524288 | tf_op jit(solution)/shard_map/all_to_all | solution.py:202
  68.1 0.0 collective-permute-start.1
  68.1 1.5 %collective-permute-done.1 = bf16[16,64,128]{2,1,0:T(8,128)(2,1)S(1)} collective-permute-done((bf16[16,64,128]{2,1,0:T(8,128)(2,1)S(1)}, bf16[16,64,128]{2,1,0:T(8,128)(2,1)S(1)}, u32[]{:S(2)}, u32[]{:S(2)}) %collective-permute-start.1) | collective-permute-done | bytes 262176 | tf_op jit(solution)/shard_map/ppermute | solution.py:207
  69.6 0.0 copy-done.1
  69.6 0.7 copy-done.5
  70.3 3.3 %step1.1 = (f32[8,8,256]{2,1,0:T(8,128)}, bf16[16,64,128]{2,1,0:T(8,128)(2,1)}) custom-call(s32[32]{0:T(128)} %reshape.40.time_ref, s32[1]{0:T(128)S(6)} %copy.17.anchor_ref, s32[1]{0:T(128)} %bitcast.1.core_ref, bf16[8,256,256]{2,1,0:T(8,128)(2,1)} %copy-done, bf16[8,2,8,8,128]{4,3,2,1,0:T(8,128)(2,1)} %bitcast.30, bf16[8,2,8,8,128]{4,3,2,1,0:T(8,128)(2,1)} %bitcast.34, ...), custom_call_target="tpu_custom_call" | custom-call | tf_op jit(solution)/shard_map/step1/pallas_call | solution.py:217
  73.7 13.9 %all_to_all.21 = bf16[16,64,128]{2,1,0:T(8,128)(2,1)S(1)} all-to-all(bf16[16,64,128]{2,1,0:T(8,128)(2,1)} %get-tuple-element.11), channel_id=1, replica_groups=mesh['hist'=8,'x'=2,'c'=2] {'hist','x'}, dimensions={0} | all-to-all | bytes 524288 | tf_op jit(solution)/shard_map/all_to_all | solution.py:202
  87.6 0.0 collective-permute-start.2
  87.6 1.5 %collective-permute-done.2 = bf16[16,64,128]{2,1,0:T(8,128)(2,1)S(1)} collective-permute-done((bf16[16,64,128]{2,1,0:T(8,128)(2,1)S(1)}, bf16[16,64,128]{2,1,0:T(8,128)(2,1)S(1)}, u32[]{:S(2)}, u32[]{:S(2)}) %collective-permute-start.2) | collective-permute-done | bytes 262176 | tf_op jit(solution)/shard_map/ppermute | solution.py:207
  89.1 0.7 copy-done.7
  89.8 3.1 %step2.1 = f32[8,8,256]{2,1,0:T(8,128)} custom-call(s32[32]{0:T(128)} %reshape.40.time_ref, s32[1]{0:T(128)S(6)} %copy.17.anchor_ref, s32[1]{0:T(128)} %bitcast.1.core_ref, bf16[8,256,256]{2,1,0:T(8,128)(2,1)} %copy-done, bf16[8,2,8,8,128]{4,3,2,1,0:T(8,128)(2,1)} %bitcast.33, bf16[8,2,8,8,128]{4,3,2,1,0:T(8,128)(2,1)} %bitcast.36, ...), custom_call_target="tpu_custom_call" | custom-call | tf_op jit(solution)/shard_map/step2/pallas_call | solution.py:217
  (17 shorter events, 0.1 us)
Async XLA Ops:
  1.8 19.7 %all-to-all-start = ((bf16[16,80,128]{2,1,0:T(8,128)(2,1)}), bf16[16,80,128]{2,1,0:T(8,128)(2,1)S(1)}, u32[]{:S(2)}, u32[]{:S(2)}) async-start(bf16[16,80,128]{2,1,0:T(8,128)(2,1)} %first.1), calls=%async_computation | async-start | bytes 655360 | tf_op jit(solution)/shard_map/all_to_all | solution.py:202
  13.1 11.9 %copy-start.4 = (f32[3,2,64,64]{3,2,1,0:T(8,128)S(1)}, f32[3,2,64,64]{3,2,1,0:T(8,128)}, u32[]{:S(2)}) copy-start(f32[3,2,64,64]{3,2,1,0:T(8,128)} %param.9) | copy-start | bytes 294916
  21.4 28.8 %all-to-all-start.1 = ((bf16[8,256,256]{2,1,0:T(8,128)(2,1)}), bf16[8,256,256]{2,1,0:T(8,128)(2,1)S(1)}, u32[]{:S(2)}, u32[]{:S(2)}) async-start(bf16[8,256,256]{2,1,0:T(8,128)(2,1)} %pack.1), calls=%async_computation.1 | async-start | bytes 2097152 | tf_op jit(solution)/shard_map/all_to_all | solution.py:182
  25.2 25.1 %copy-start.2 = (bf16[16,64,128]{2,1,0:T(8,128)(2,1)}, bf16[16,64,128]{2,1,0:T(8,128)(2,1)S(1)}, u32[]{:S(2)}) copy-start(bf16[16,64,128]{2,1,0:T(8,128)(2,1)S(1)} %slice.29) | copy-start | bytes 786436
  25.2 2.1 %collective-permute-start = (bf16[16,64,128]{2,1,0:T(8,128)(2,1)S(1)}, bf16[16,64,128]{2,1,0:T(8,128)(2,1)S(1)}, u32[]{:S(2)}, u32[]{:S(2)}) collective-permute-start(bf16[16,64,128]{2,1,0:T(8,128)(2,1)S(1)} %slice.29), channel_id=1, source_target_pairs={{0,1},{1,0},{2,3},{3,2},{4,5},{5,4},{6,7},{7,6},{8,9},{9,8},{10,11... | collective-permute-start | bytes 786440 | tf_op jit(solution)/shard_map/ppermute | solution.py:207
  27.3 23.0 %copy-start.6 = (bf16[16,64,128]{2,1,0:T(8,128)(2,1)}, bf16[16,64,128]{2,1,0:T(8,128)(2,1)S(1)}, u32[]{:S(2)}) copy-start(bf16[16,64,128]{2,1,0:T(8,128)(2,1)S(1)} %collective-permute-done) | copy-start | bytes 786436
  50.3 1.0 %copy-start = (bf16[8,256,256]{2,1,0:T(8,128)(2,1)}, bf16[8,256,256]{2,1,0:T(8,128)(2,1)S(1)}, u32[]{:S(2)}) copy-start(bf16[8,256,256]{2,1,0:T(8,128)(2,1)S(1)} %all-to-all-done.1.hist_ref) | copy-start | bytes 3145732
  68.1 1.5 %copy-start.1 = (bf16[16,64,128]{2,1,0:T(8,128)(2,1)}, bf16[16,64,128]{2,1,0:T(8,128)(2,1)S(1)}, u32[]{:S(2)}) copy-start(bf16[16,64,128]{2,1,0:T(8,128)(2,1)S(1)} %all_to_all.20) | copy-start | bytes 786436
  68.1 1.5 %collective-permute-start.1 = (bf16[16,64,128]{2,1,0:T(8,128)(2,1)S(1)}, bf16[16,64,128]{2,1,0:T(8,128)(2,1)S(1)}, u32[]{:S(2)}, u32[]{:S(2)}) collective-permute-start(bf16[16,64,128]{2,1,0:T(8,128)(2,1)S(1)} %all_to_all.20), channel_id=1, source_target_pairs={{0,1},{1,0},{2,3},{3,2},{4,5},{5,4},{6,7},{7,6},{8,9},{9,8},{10,11... | collective-permute-start | bytes 786440 | tf_op jit(solution)/shard_map/ppermute | solution.py:207
  69.6 0.7 copy-start.5
  87.6 1.5 %copy-start.3 = (bf16[16,64,128]{2,1,0:T(8,128)(2,1)}, bf16[16,64,128]{2,1,0:T(8,128)(2,1)S(1)}, u32[]{:S(2)}) copy-start(bf16[16,64,128]{2,1,0:T(8,128)(2,1)S(1)} %all_to_all.21) | copy-start | bytes 786436
  87.6 1.5 %collective-permute-start.2 = (bf16[16,64,128]{2,1,0:T(8,128)(2,1)S(1)}, bf16[16,64,128]{2,1,0:T(8,128)(2,1)S(1)}, u32[]{:S(2)}, u32[]{:S(2)}) collective-permute-start(bf16[16,64,128]{2,1,0:T(8,128)(2,1)S(1)} %all_to_all.21), channel_id=1, source_target_pairs={{0,1},{1,0},{2,3},{3,2},{4,5},{5,4},{6,7},{7,6},{8,9},{9,8},{10,11... | collective-permute-start | bytes 786440 | tf_op jit(solution)/shard_map/ppermute | solution.py:207
  89.1 0.7 copy-start.7

commit v2 on v1

v2 whole, which is shorter than its diff:
```python
import functools

import jax
import jax.numpy as jnp
from jax import lax
from jax.experimental import pallas as pl
from jax.experimental.pallas import tpu as pltpu
from jax.sharding import Mesh, PartitionSpec as P


step_width = 0.05
highest = lax.Precision.HIGHEST
bf16 = jnp.bfloat16
f32 = jnp.float32
vmem = pl.BlockSpec(memory_space=pltpu.VMEM)
smem = pl.BlockSpec(memory_space=pltpu.SMEM)
params = pltpu.CompilerParams(vmem_limit_bytes=16 * 2**20)


def local(x):
    return pltpu.with_memory_space_constraint(x, pltpu.VMEM)


def pack_kernel(groups, place_ref, hist_ref, *rest):
    out_refs, (wide_ref, turned_ref) = rest[:-2], rest[-2:]
    rows = hist_ref.shape[0] // groups
    width = hist_ref.shape[1] // len(out_refs)
    wide_ref[...] = hist_ref[...].astype(f32)
    for group in range(groups):
        turned = wide_ref[pl.ds(group, rows, stride=groups), :].T
        for peer in range(len(out_refs)):
            turned_ref[group % 2, peer] = turned[peer * width : (peer + 1) * width]
        for offset, out_ref in enumerate(out_refs):
            out_ref[group * width : (group + 1) * width, :] = turned_ref[
                group % 2, place_ref[0] ^ offset
            ].astype(bf16)


def cubic_term(first_real, first_imag, other_real, other_imag):
    square_real = first_real * first_real - first_imag * first_imag
    square_imag = 2.0 * first_real * first_imag
    return (
        square_real * other_real + square_imag * other_imag,
        square_imag * other_real - square_real * other_imag,
    )


def energy_of(lesser, greater, weight_sq):
    half = lesser.shape[-1] // 2
    lr, li = lesser[:, :half], lesser[:, half:]
    gr, gi = greater[:, :half], greater[:, half:]
    less_real, less_imag = cubic_term(lr, li, gr, gi)
    more_real, more_imag = cubic_term(gr, gi, lr, li)
    return jnp.concatenate(
        [weight_sq * (more_real - less_real), weight_sq * (more_imag - less_imag)], axis=-1
    )


def send_energy(row_ref, coupling_ref, scratch_ref, send_ref):
    own_rows, slab, lanes = row_ref.shape
    for b in range(own_rows):
        row = row_ref[b]
        weight = coupling_ref[b : b + 1, :]
        scratch_ref[pl.ds(b, slab, stride=own_rows), :] = energy_of(
            row[:, : lanes // 2], row[:, lanes // 2 :], weight * weight
        )
    for t in range(slab):
        narrow = scratch_ref[t * own_rows : (t + 1) * own_rows, :].astype(bf16)
        for peer in range(send_ref.shape[0]):
            send_ref[peer, t] = narrow


def first_kernel(row_ref, coupling_ref, time_ref, send_ref, scratch_ref):
    slab, own_rows, lanes = row_ref.shape[1], row_ref.shape[0], send_ref.shape[3]
    send_energy(row_ref, coupling_ref, scratch_ref, send_ref)
    lane = lax.broadcasted_iota(jnp.int32, (own_rows, lanes), 1)
    times = jnp.zeros((own_rows, lanes), jnp.int32)
    for slot in range(time_ref.shape[0]):
        times = jnp.where(lane == slot, time_ref[slot], times)
    narrow = times.astype(f32).astype(bf16)
    for peer in range(send_ref.shape[0]):
        send_ref[peer, slab] = narrow


def prepare_kernel(row_ref, high_ref, low_ref):
    row = row_ref[...]
    high = row.astype(bf16)
    high_ref[...] = high
    low_ref[...] = (row - high.astype(f32)).astype(bf16)


def step_kernel(
    peers, n_past, relative, last, time_ref, anchor_ref, place_ref, own_ref, other_ref, row_ref, *rest
):
    hist_refs, rest = rest[:peers], rest[peers:]
    past_refs = rest[: 2 * n_past]
    inverse_ref, coupling_ref, out_ref = rest[2 * n_past : 2 * n_past + 3]
    rest = rest[2 * n_past + 3 :]
    if last:
        chosen_ref, sum_ref = rest
        send_ref = energy_ref = None
    else:
        send_ref, chosen_ref, sum_ref, energy_ref = rest
    own_rows, lanes = own_ref.shape[3], own_ref.shape[4]
    slab = row_ref.shape[1]
    orbitals = peers * own_rows
    half = lanes // 2
    slots = time_ref.shape[0]
    block = slots // peers
    anchor = anchor_ref[0]
    hist_place, far_place, core = place_ref[0], place_ref[1], place_ref[2]

    def energy_at(time):
        inner = lax.rem(time, slab)
        group = lax.div(time, slab)
        far = lax.div(group, 2)
        same = lax.rem(group, 2) == core
        parts = []
        for peer in range(peers):
            place = far ^ far_place if relative else far
            parts.append(jnp.where(same, own_ref[peer, place, inner], other_ref[peer, place, inner]))
        return parts

    def choose(source, slot):
        time = time_ref[(source ^ hist_place) * block + slot]
        alive = time <= anchor
        for peer, part in enumerate(energy_at(time)):
            chosen_ref[source * block + slot, peer * own_rows : (peer + 1) * own_rows, :] = (
                jnp.where(alive, part, jnp.zeros_like(part))
            )

    if slots <= 32:
        for source in range(peers):
            for slot in range(block):
                choose(source, slot)
    else:

        @pl.loop(0, peers)
        def _(source):
            for slot in range(block):
                choose(source, slot)

    total = None
    for peer in range(peers):
        part = jnp.dot(
            hist_refs[peer][...],
            chosen_ref[peer * block : (peer + 1) * block].reshape(block * orbitals, lanes),
            preferred_element_type=f32,
        )
        total = part if total is None else total + part
    sum_ref[...] = total
    sign = jnp.where(lax.broadcasted_iota(jnp.int32, (1, lanes), 1) < half, -1.0, 1.0)
    columns = []
    for past in range(n_past):
        for peer, part in enumerate(energy_at(anchor + 1 + past)):
            chosen_ref[past, peer * own_rows : (peer + 1) * own_rows, :] = part
        columns.append(chosen_ref[past])
    for m in range(2):
        evens, odds = [], []
        for b in range(own_rows):
            first = m * 2 * own_rows + 2 * b
            evens.append(sum_ref[pl.ds(first, slab, stride=4 * own_rows), :])
            odds.append(sum_ref[pl.ds(first + 1, slab, stride=4 * own_rows), :])
        even = jnp.concatenate(evens, axis=0)
        odd = jnp.concatenate(odds, axis=0)
        for past, column in enumerate(columns):
            for past_ref in past_refs[2 * past : 2 * past + 2]:
                start = m * lanes
                even += jnp.dot(
                    past_ref[:, start : start + half], column, preferred_element_type=f32
                )
                odd += jnp.dot(
                    past_ref[:, start + half : start + lanes], column, preferred_element_type=f32
                )
        integral = even + sign * pltpu.roll(odd, half, 1)
        row = row_ref[:, :, m * lanes : (m + 1) * lanes].reshape(own_rows * slab, lanes)
        moved = lax.dot_general(
            row + step_width * integral,
            inverse_ref[...],
            (((1,), (1,)), ((), ())),
            precision=highest,
            preferred_element_type=f32,
        )
        out_ref[:, :, m * lanes : (m + 1) * lanes] = moved.reshape(own_rows, slab, lanes)
    if not last:
        send_energy(out_ref, coupling_ref, energy_ref, send_ref)


def spread(block, axis):
    size = lax.axis_size(axis)
    gathered = block[None]
    stride = size // 2
    while stride:
        ring = [(i, i ^ stride) for i in range(size)]
        other = lax.ppermute(gathered, axis, ring)
        gathered = jnp.stack([gathered, other], axis=1).reshape(-1, *block.shape)
        stride //= 2
    return gathered


def body(history, row_now, coupling, step_inverse, start_step, history_time):
    slots_dev, orbitals, slab, parts, lanes = history.shape
    own_rows = row_now.shape[0]
    steps = step_inverse.shape[0]
    peers = lax.axis_size("hist")
    far = lax.axis_size("x")
    groups = slab * parts
    width = lanes // peers
    n_sum = groups * width
    rows = slab * own_rows
    place = jnp.stack([lax.axis_index(name) for name in ("hist", "x", "c")])
    packed = pl.pallas_call(
        functools.partial(pack_kernel, groups),
        out_shape=[pltpu.VMEM((n_sum, slots_dev * orbitals), bf16)] * peers,
        in_specs=[smem, vmem],
        out_specs=[vmem] * peers,
        scratch_shapes=[
            pltpu.VMEM((slots_dev * orbitals * groups, lanes), f32),
            pltpu.VMEM((2, peers, width, slots_dev * orbitals), f32),
        ],
        compiler_params=params,
        name="pack",
    )(place, history.reshape(slots_dev * orbitals * groups, lanes))
    sent = pl.pallas_call(
        first_kernel,
        out_shape=pltpu.VMEM((peers, slab + 1, own_rows, lanes), bf16),
        in_specs=[vmem, vmem, smem],
        out_specs=vmem,
        scratch_shapes=[pltpu.VMEM((rows, lanes), f32)],
        compiler_params=params,
        name="first",
    )(row_now, coupling, history_time)
    moved = [packed[0]]
    for offset in range(1, peers):
        ring = [(i, i ^ offset) for i in range(peers)]
        moved.append(lax.ppermute(packed[offset], "hist", ring))
    real, imag = step_inverse[:, 0], step_inverse[:, 1]
    inverse = jnp.concatenate(
        [jnp.concatenate([real, -imag], axis=2), jnp.concatenate([imag, real], axis=2)], axis=1
    )
    green, past = row_now, []
    times = None
    for w in range(steps):
        last = w == steps - 1
        if w == 0:
            own = lax.all_to_all(sent, "hist", split_axis=0, concat_axis=0, tiled=True)
            times = own[:, slab, 0, :slots_dev].astype(jnp.int32).reshape(peers * slots_dev)
            own = spread(own, "x").swapaxes(0, 1)
        else:
            own = lax.all_to_all(sent, ("hist", "x"), split_axis=0, concat_axis=0, tiled=True)
            own = own.reshape(peers, far, slab, own_rows, lanes)
            past += pl.pallas_call(
                prepare_kernel,
                out_shape=[pltpu.VMEM((rows, 2 * lanes), bf16)] * 2,
                in_specs=[vmem],
                out_specs=[vmem] * 2,
                compiler_params=params,
            )(local(green.reshape(rows, 2 * lanes)))
        other = lax.ppermute(own, "c", [(0, 1), (1, 0)])
        scratch = [
            pltpu.VMEM((peers * slots_dev, orbitals, lanes), bf16),
            pltpu.VMEM((n_sum, lanes), f32),
        ]
        if last:
            outs = [jax.ShapeDtypeStruct(row_now.shape, f32)]
        else:
            outs = [
                pltpu.VMEM(row_now.shape, f32),
                pltpu.VMEM((peers * far, slab, own_rows, lanes), bf16),
            ]
            scratch.append(pltpu.VMEM((rows, lanes), f32))
        result = pl.pallas_call(
            functools.partial(step_kernel, peers, len(past) // 2, w == 0, last),
            out_shape=outs,
            in_specs=[smem] * 3 + [vmem] * (5 + peers + len(past)),
            out_specs=[vmem] * len(outs),
            scratch_shapes=scratch,
            compiler_params=params,
        )(
            times,
            start_step,
            place,
            local(own),
            local(other),
            local(green),
            *[local(block) for block in moved],
            *[local(row) for row in past],
            local(inverse[w]),
            local(coupling),
        )
        green = result[0]
        if not last:
            sent = result[1]
    return green


def solution(mesh):
    n_hist, n_second = mesh.devices.shape
    split = Mesh(mesh.devices.reshape(n_hist, n_second // 2, 2), ("hist", "x", "c"))
    second = ("x", "c")
    placed = (
        P("hist", None, second, None, None),
        P("hist", second, None),
        P("hist", None),
        P(),
        P(),
        P("hist"),
    )
    return jax.shard_map(
        body, mesh=split, in_specs=placed, out_specs=P("hist", second, None), check_vma=False
    )
```

time: 93.5 us -> 80.9 us (0.87)
  waiting for transfers between devices: 34.4 us -> 14.9 us
  starting transfers between devices: 12 us -> 20.2 us
  Pallas kernels: 14.5 us -> 9.06 us
  blocking collectives: 27.4 us -> 31.8 us
    all_to_all x2 -> x1, waiting for transfers between devices: 31.3 us -> 0.01 us  [body(): own = lax.all_to_all(sent, 'hist', split_axis=0, concat_axis=0, tiled=True)]
    ppermute x0 -> x8, starting transfers between devices: none -> 12.9 us  [the longest x7 11.4 us: body(): moved.append(lax.ppermute(packed[offset], 'hist', ring))]
    ppermute x0 -> x8, waiting for transfers between devices: none -> 11.9 us  [the longest x7 8.37 us: body(): moved.append(lax.ppermute(packed[offset], 'hist', ring))]
    pallas_call x5 -> x7, Pallas kernels: 14.5 us -> 9.06 us  [the longest x3 5.85 us: body(): pl.pallas_call(functools.partial(step_kernel, peers, len(past) // 2, w ==...]
    all_to_all x2 -> x1, starting transfers between devices: 11.9 us -> 7.31 us  [body(): own = lax.all_to_all(sent, 'hist', split_axis=0, concat_axis=0, tiled=True)]
    all_to_all x2, blocking collectives: 27.4 us -> 31.8 us  [body(): lax.all_to_all(sent, ('hist', 'x'), split_axis=0, concat_axis=0, tiled=True)]
    unnamed x16 -> x14, local copies, waits for them, and re-layouts: 2.39 us -> 3.42 us
  transfers between devices with their start and end apart: 5 -> 12, of which waited for: 4 -> 4; matrix products, arithmetic and copies ran while one was open for 2% -> 0% of each run, Pallas kernels for 3% -> 2%
where the time goes in v2:
time: 80.9 us; the launch traced here: 80.5 us
  blocking collectives  31.8 us (39%)
  starting transfers between devices  20.2 us (25%)
  waiting for transfers between devices  14.9 us (18%)
  Pallas kernels  9.06 us (11%)
  local copies, waits for them, and re-layouts  3.53 us (4%)
    all_to_all x2, blocking collectives, body(): lax.all_to_all(sent, ('hist', 'x'), split_axis=0, concat_axis=0, tiled=True)  31.8 us
    ppermute x7, starting transfers between devices, body(): moved.append(lax.ppermute(packed[offset], 'hist', ring))  11.4 us
    ppermute x7, waiting for transfers between devices, body(): moved.append(lax.ppermute(packed[offset], 'hist', ring))  8.37 us
    all_to_all x1, starting transfers between devices, body(): own = lax.all_to_all(sent, 'hist', split_axis=0, concat_axis=0, tiled=True)  7.31 us
    pallas_call x3, Pallas kernels, body(): pl.pallas_call(functools.partial(step_kernel, peers, len(past) // 2, w ==...  5.85 us
    ppermute x1, waiting for transfers between devices, spread(): other = lax.ppermute(gathered, axis, ring)  3.52 us
    unnamed x14, local copies, waits for them, and re-layouts  3.42 us
    ppermute x3, waiting for transfers between devices, body(): other = lax.ppermute(own, 'c', [(0, 1), (1, 0)])  3.04 us
  transfers between devices with their start and end apart: 12, of which 4 were waited for; matrix products, arithmetic and copies ran while one was open for 0% of the time, Pallas kernels for 2%

profile of v2, /device:TPU:0, one launch (start us, length us, event | category | flops | bytes accessed | tf_op | source)
XLA Modules:
  0.0 80.5 jit_solution(3156639463474326258)
XLA Ops:
  0.0 0.8 %copy-done.1 = f32[8,8,256]{2,1,0:T(8,128)S(1)} copy-done((f32[8,8,256]{2,1,0:T(8,128)S(1)}, f32[8,8,256]{2,1,0:T(8,128)}, u32[]{:S(2)}) %copy-start.1) | copy-done | bytes 65560
  0.8 0.7 copy-done.3
  1.5 0.7 copy-done.5
  2.2 1.4 %first.1 = bf16[8,9,8,128]{3,2,1,0:T(8,128)(2,1)} custom-call(f32[8,8,256]{2,1,0:T(8,128)S(1)} %copy-done.1, f32[8,64]{1,0:T(8,128)S(1)} %copy-done.3, s32[4]{0:T(128)S(1)} %copy-done.5), custom_call_target="tpu_custom_call" | custom-call | tf_op jit(solution)/shard_map/first/pallas_call | solution.py:224
  3.6 7.3 %all-to-all-start = ((bf16[8,9,8,128]{3,2,1,0:T(8,128)(2,1)}), bf16[8,9,8,128]{3,2,1,0:T(8,128)(2,1)S(1)}, u32[]{:S(2)}, u32[]{:S(2)}) async-start(bf16[8,9,8,128]{3,2,1,0:T(8,128)(2,1)} %first.1), calls=%async_computation | async-start | bytes 294912 | tf_op jit(solution)/shard_map/all_to_all | solution.py:246
  11.0 1.2 %copy-done = bf16[4,64,8,2,128]{4,3,2,1,0:T(2,128)(2,1)S(1)} copy-done((bf16[4,64,8,2,128]{4,3,2,1,0:T(2,128)(2,1)S(1)}, bf16[4,64,8,2,128]{4,3,2,1,0:T(2,128)(2,1)}, u32[]{:S(2)}) %copy-start) | copy-done | bytes 1048600
  12.2 1.8 %pack.1 = (bf16[256,256]{1,0:T(8,128)(2,1)S(1)}, bf16[256,256]{1,0:T(8,128)(2,1)S(1)}, bf16[256,256]{1,0:T(8,128)(2,1)S(1)}, bf16[256,256]{1,0:T(8,128)(2,1)S(1)...) custom-call(s32[3]{0:T(128)S(1)} %pad_add_fusion.place_ref, ...), custom_call_target="tpu_custom_call" | custom-call | tf_op jit(solution)/shard_map/pack/pallas_call | solution.py:212
  14.0 2.1 %collective-permute-start.2 = (bf16[256,256]{1,0:T(8,128)(2,1)S(1)}, bf16[256,256]{1,0:T(8,128)(2,1)S(1)}, u32[]{:S(2)}, u32[]{:S(2)}) collective-permute-start(bf16[256,256]{1,0:T(8,128)(2,1)S(1)} %get-tuple-element.22), channel_id=1, source_target_pairs={{0,4},{4,0},{8,12},{12,8},{16,20},{20,16},{24,28},{28,24},{1,5},{5... | collective-permute-start | bytes 393224 | tf_op jit(solution)/shard_map/ppermute | solution.py:236
  16.1 1.5 %collective-permute-start.3 = (bf16[256,256]{1,0:T(8,128)(2,1)S(1)}, bf16[256,256]{1,0:T(8,128)(2,1)S(1)}, u32[]{:S(2)}, u32[]{:S(2)}) collective-permute-start(bf16[256,256]{1,0:T(8,128)(2,1)S(1)} %get-tuple-element.23), channel_id=1, source_target_pairs={{0,8},{4,12},{8,0},{12,4},{16,24},{20,28},{24,16},{28,20},{1,9},{5... | collective-permute-start | bytes 393224 | tf_op jit(solution)/shard_map/ppermute | solution.py:236
  17.6 2.8 %collective-permute-start.5 = (bf16[256,256]{1,0:T(8,128)(2,1)S(1)}, bf16[256,256]{1,0:T(8,128)(2,1)S(1)}, u32[]{:S(2)}, u32[]{:S(2)}) collective-permute-start(bf16[256,256]{1,0:T(8,128)(2,1)S(1)} %get-tuple-element.25), channel_id=1, source_target_pairs={{0,16},{4,20},{8,24},{12,28},{16,0},{20,4},{24,8},{28,12},{1,17},{... | collective-permute-start | bytes 393224 | tf_op jit(solution)/shard_map/ppermute | solution.py:236
  20.5 1.6 %collective-permute-start = (bf16[1,8,9,8,128]{4,3,2,1,0:T(8,128)(2,1)S(1)}, bf16[1,8,9,8,128]{4,3,2,1,0:T(8,128)(2,1)S(1)}, u32[]{:S(2)}, u32[]{:S(2)}) collective-permute-start(bf16[1,8,9,8,128]{4,3,2,1,0:T(8,128)(2,1)S(1)} %bitcast.40), channel_id=1, source_target_pairs={{0,2},{2,0},{1,3},{3,1},{4,6},{6,4},{5,7},{7,5},{8,10},{10,8},{9,1... | collective-permute-start | bytes 442376 | tf_op jit(solution)/shard_map/ppermute | solution.py:195
  22.1 0.1 maximum_maximum_fusion
  22.2 3.5 %collective-permute-done = bf16[1,8,9,8,128]{4,3,2,1,0:T(8,128)(2,1)S(1)} collective-permute-done((bf16[1,8,9,8,128]{4,3,2,1,0:T(8,128)(2,1)S(1)}, bf16[1,8,9,8,128]{4,3,2,1,0:T(8,128)(2,1)S(1)}, u32[]{:S(2)}, u32[]{:S(2)}) %collective-permute-start) | collective-permute-done | bytes 147488 | tf_op jit(solution)/shard_map/ppermute | solution.py:195
  25.7 1.5 %collective-permute-start.6 = (bf16[256,256]{1,0:T(8,128)(2,1)S(1)}, bf16[256,256]{1,0:T(8,128)(2,1)S(1)}, u32[]{:S(2)}, u32[]{:S(2)}) collective-permute-start(bf16[256,256]{1,0:T(8,128)(2,1)S(1)} %get-tuple-element.26), channel_id=1, source_target_pairs={{0,20},{4,16},{8,28},{12,24},{16,4},{20,0},{24,12},{28,8},{1,21},{... | collective-permute-start | bytes 393224 | tf_op jit(solution)/shard_map/ppermute | solution.py:236
  27.2 3.3 %collective-permute-start.7 = (bf16[256,256]{1,0:T(8,128)(2,1)S(1)}, bf16[256,256]{1,0:T(8,128)(2,1)S(1)}, u32[]{:S(2)}, u32[]{:S(2)}) collective-permute-start(bf16[256,256]{1,0:T(8,128)(2,1)S(1)} %get-tuple-element.27), channel_id=1, source_target_pairs={{0,24},{4,28},{8,16},{12,20},{16,8},{20,12},{24,0},{28,4},{1,25},{... | collective-permute-start | bytes 393224 | tf_op jit(solution)/shard_map/ppermute | solution.py:236
  30.5 0.1 collective-permute-start.8
  31.4 8.4 %collective-permute-done.6.rest_5_ = bf16[256,256]{1,0:T(8,128)(2,1)S(1)} collective-permute-done((bf16[256,256]{1,0:T(8,128)(2,1)S(1)}, bf16[256,256]{1,0:T(8,128)(2,1)S(1)}, u32[]{:S(2)}, u32[]{:S(2)}) %collective-permute-start.6) | collective-permute-done | bytes 131104 | tf_op jit(solution)/shard_map/ppermute | solution.py:236
  39.8 1.8 %shard_map.64 = (f32[8,8,256]{2,1,0:T(8,128)S(1)}, bf16[16,8,8,128]{3,2,1,0:T(8,128)(2,1)S(1)}) custom-call(s32[32]{0:T(128)S(1)} %reshape.28.time_ref, s32[1]{0:T(128)S(6)} %copy.15.anchor_ref, s32[3]{0:T(128)S(1)} %pad_add_fusion.place_ref, bf16[8,2,9,8,128]{4,3,2,1,0:T(8,128)(2,1)S(1)} %maximum_bitcast_fusion.own_ref, ...), custom_call_target="tpu_custom_call" | custom-call | tf_op jit(solution)/shard_map/pallas_call | solution.py:272
  41.6 18.2 %all_to_all.15 = bf16[16,8,8,128]{3,2,1,0:T(8,128)(2,1)S(1)} all-to-all(bf16[16,8,8,128]{3,2,1,0:T(8,128)(2,1)S(1)} %get-tuple-element.29), channel_id=1, replica_groups=mesh['hist'=8,'x'=2,'c'=2] {'hist','x'}, dimensions={0} | all-to-all | bytes 524288 | tf_op jit(solution)/shard_map/all_to_all | solution.py:250
  59.9 1.5 %collective-permute-done.9.other_ref = bf16[8,2,8,8,128]{4,3,2,1,0:T(8,128)(2,1)S(1)} collective-permute-done((bf16[8,2,8,8,128]{4,3,2,1,0:T(8,128)(2,1)S(1)}, bf16[8,2,8,8,128]{4,3,2,1,0:T(8,128)(2,1)S(1)}, u32[]{:S(2)}, u32[]{:S(2)}) %collective-permute-start.9) | collective-permute-done | bytes 262176 | tf_op jit(solution)/shard_map/ppermute | solution.py:259
  61.4 1.8 %shard_map.66 = (f32[8,8,256]{2,1,0:T(8,128)S(1)}, bf16[16,8,8,128]{3,2,1,0:T(8,128)(2,1)S(1)}) custom-call(s32[32]{0:T(128)S(1)} %reshape.28.time_ref, s32[1]{0:T(128)S(6)} %copy.15.anchor_ref, s32[3]{0:T(128)S(1)} %pad_add_fusion.place_ref, bf16[8,2,8,8,128]{4,3,2,1,0:T(8,128)(2,1)S(1)} %bitcast.34, ...), custom_call_target="tpu_custom_call" | custom-call | tf_op jit(solution)/shard_map/pallas_call | solution.py:272
  63.2 13.5 %all_to_all.16 = bf16[16,8,8,128]{3,2,1,0:T(8,128)(2,1)S(1)} all-to-all(bf16[16,8,8,128]{3,2,1,0:T(8,128)(2,1)S(1)} %get-tuple-element.33), channel_id=1, replica_groups=mesh['hist'=8,'x'=2,'c'=2] {'hist','x'}, dimensions={0} | all-to-all | bytes 524288 | tf_op jit(solution)/shard_map/all_to_all | solution.py:250
  76.7 1.5 %collective-permute-done.10.other_ref = bf16[8,2,8,8,128]{4,3,2,1,0:T(8,128)(2,1)S(1)} collective-permute-done((bf16[8,2,8,8,128]{4,3,2,1,0:T(8,128)(2,1)S(1)}, bf16[8,2,8,8,128]{4,3,2,1,0:T(8,128)(2,1)S(1)}, u32[]{:S(2)}, u32[]{:S(2)}) %collective-permute-start.10) | collective-permute-done | bytes 262176 | tf_op jit(solution)/shard_map/ppermute | solution.py:259
  78.3 2.3 %shard_map.68 = f32[8,8,256]{2,1,0:T(8,128)} custom-call(s32[32]{0:T(128)S(1)} %reshape.28.time_ref, s32[1]{0:T(128)S(6)} %copy.15.anchor_ref, s32[3]{0:T(128)S(1)} %pad_add_fusion.place_ref, bf16[8,2,8,8,128]{4,3,2,1,0:T(8,128)(2,1)S(1)} %bitcast.37, bf16[8,2,8,8,128]{4,3,2,1,0:T(8,128)(2,1)S(1)} %collective-permute-done.10.other_ref, ...), custom_call_target="tpu_custom_call" | custom-call | tf_op jit(solution)/shard_map/pallas_call | solution.py:272
  (31 shorter events, 0.4 us)
Async XLA Ops:
  0.0 0.8 %copy-start.1 = (f32[8,8,256]{2,1,0:T(8,128)S(1)}, f32[8,8,256]{2,1,0:T(8,128)}, u32[]{:S(2)}) copy-start(f32[8,8,256]{2,1,0:T(8,128)} %row_ref.3) | copy-start | bytes 196612
  0.8 0.7 copy-start.3
  1.5 0.7 copy-start.5
  3.6 16.9 %all-to-all-start = ((bf16[8,9,8,128]{3,2,1,0:T(8,128)(2,1)}), bf16[8,9,8,128]{3,2,1,0:T(8,128)(2,1)S(1)}, u32[]{:S(2)}, u32[]{:S(2)}) async-start(bf16[8,9,8,128]{3,2,1,0:T(8,128)(2,1)} %first.1), calls=%async_computation | async-start | bytes 294912 | tf_op jit(solution)/shard_map/all_to_all | solution.py:246
  11.0 1.2 %copy-start = (bf16[4,64,8,2,128]{4,3,2,1,0:T(2,128)(2,1)S(1)}, bf16[4,64,8,2,128]{4,3,2,1,0:T(2,128)(2,1)}, u32[]{:S(2)}) copy-start(bf16[4,64,8,2,128]{4,3,2,1,0:T(2,128)(2,1)} %param.6) | copy-start | bytes 3145732
  12.2 8.3 %copy-start.6 = (f32[3,2,64,64]{3,2,1,0:T(8,128)S(1)}, f32[3,2,64,64]{3,2,1,0:T(8,128)}, u32[]{:S(2)}) copy-start(f32[3,2,64,64]{3,2,1,0:T(8,128)} %param.9) | copy-start | bytes 294916
  14.0 13.2 %collective-permute-start.2 = (bf16[256,256]{1,0:T(8,128)(2,1)S(1)}, bf16[256,256]{1,0:T(8,128)(2,1)S(1)}, u32[]{:S(2)}, u32[]{:S(2)}) collective-permute-start(bf16[256,256]{1,0:T(8,128)(2,1)S(1)} %get-tuple-element.22), channel_id=1, source_target_pairs={{0,4},{4,0},{8,12},{12,8},{16,20},{20,16},{24,28},{28,24},{1,5},{5... | collective-permute-start | bytes 393224 | tf_op jit(solution)/shard_map/ppermute | solution.py:236
  16.1 14.5 %collective-permute-start.3 = (bf16[256,256]{1,0:T(8,128)(2,1)S(1)}, bf16[256,256]{1,0:T(8,128)(2,1)S(1)}, u32[]{:S(2)}, u32[]{:S(2)}) collective-permute-start(bf16[256,256]{1,0:T(8,128)(2,1)S(1)} %get-tuple-element.23), channel_id=1, source_target_pairs={{0,8},{4,12},{8,0},{12,4},{16,24},{20,28},{24,16},{28,20},{1,9},{5... | collective-permute-start | bytes 393224 | tf_op jit(solution)/shard_map/ppermute | solution.py:236
  17.5 13.1 %collective-permute-start.4 = (bf16[256,256]{1,0:T(8,128)(2,1)S(1)}, bf16[256,256]{1,0:T(8,128)(2,1)S(1)}, u32[]{:S(2)}, u32[]{:S(2)}) collective-permute-start(bf16[256,256]{1,0:T(8,128)(2,1)S(1)} %get-tuple-element.24), channel_id=1, source_target_pairs={{0,12},{4,8},{8,4},{12,0},{16,28},{20,24},{24,20},{28,16},{1,13},{... | collective-permute-start | bytes 393224 | tf_op jit(solution)/shard_map/ppermute | solution.py:236
  17.6 13.8 %collective-permute-start.5 = (bf16[256,256]{1,0:T(8,128)(2,1)S(1)}, bf16[256,256]{1,0:T(8,128)(2,1)S(1)}, u32[]{:S(2)}, u32[]{:S(2)}) collective-permute-start(bf16[256,256]{1,0:T(8,128)(2,1)S(1)} %get-tuple-element.25), channel_id=1, source_target_pairs={{0,16},{4,20},{8,24},{12,28},{16,0},{20,4},{24,8},{28,12},{1,17},{... | collective-permute-start | bytes 393224 | tf_op jit(solution)/shard_map/ppermute | solution.py:236
  20.5 5.2 %collective-permute-start = (bf16[1,8,9,8,128]{4,3,2,1,0:T(8,128)(2,1)S(1)}, bf16[1,8,9,8,128]{4,3,2,1,0:T(8,128)(2,1)S(1)}, u32[]{:S(2)}, u32[]{:S(2)}) collective-permute-start(bf16[1,8,9,8,128]{4,3,2,1,0:T(8,128)(2,1)S(1)} %bitcast.40), channel_id=1, source_target_pairs={{0,2},{2,0},{1,3},{3,1},{4,6},{6,4},{5,7},{7,5},{8,10},{10,8},{9,1... | collective-permute-start | bytes 442376 | tf_op jit(solution)/shard_map/ppermute | solution.py:195
  25.7 14.1 %collective-permute-start.6 = (bf16[256,256]{1,0:T(8,128)(2,1)S(1)}, bf16[256,256]{1,0:T(8,128)(2,1)S(1)}, u32[]{:S(2)}, u32[]{:S(2)}) collective-permute-start(bf16[256,256]{1,0:T(8,128)(2,1)S(1)} %get-tuple-element.26), channel_id=1, source_target_pairs={{0,20},{4,16},{8,28},{12,24},{16,4},{20,0},{24,12},{28,8},{1,21},{... | collective-permute-start | bytes 393224 | tf_op jit(solution)/shard_map/ppermute | solution.py:236
  27.2 12.6 %collective-permute-start.7 = (bf16[256,256]{1,0:T(8,128)(2,1)S(1)}, bf16[256,256]{1,0:T(8,128)(2,1)S(1)}, u32[]{:S(2)}, u32[]{:S(2)}) collective-permute-start(bf16[256,256]{1,0:T(8,128)(2,1)S(1)} %get-tuple-element.27), channel_id=1, source_target_pairs={{0,24},{4,28},{8,16},{12,20},{16,8},{20,12},{24,0},{28,4},{1,25},{... | collective-permute-start | bytes 393224 | tf_op jit(solution)/shard_map/ppermute | solution.py:236
  30.5 9.3 %copy-start.2 = (f32[8,8,256]{2,1,0:T(8,128)S(1)}, f32[8,8,256]{2,1,0:T(8,128)}, u32[]{:S(2)}) copy-start(f32[8,8,256]{2,1,0:T(8,128)} %row_ref.3) | copy-start | bytes 196612
  30.5 9.2 %collective-permute-start.8 = (bf16[256,256]{1,0:T(8,128)(2,1)S(1)}, bf16[256,256]{1,0:T(8,128)(2,1)S(1)}, u32[]{:S(2)}, u32[]{:S(2)}) collective-permute-start(bf16[256,256]{1,0:T(8,128)(2,1)S(1)} %get-tuple-element.28), channel_id=1, source_target_pairs={{0,28},{4,24},{8,20},{12,16},{16,12},{20,8},{24,4},{28,0},{1,29},{... | collective-permute-start | bytes 393224 | tf_op jit(solution)/shard_map/ppermute | solution.py:236
  30.6 9.2 %collective-permute-start.1 = (bf16[8,2,9,8,128]{4,3,2,1,0:T(8,128)(2,1)S(1)}, bf16[8,2,9,8,128]{4,3,2,1,0:T(8,128)(2,1)S(1)}, u32[]{:S(2)}, u32[]{:S(2)}) collective-permute-start(bf16[8,2,9,8,128]{4,3,2,1,0:T(8,128)(2,1)S(1)} %maximum_bitcast_fusion.own_ref), channel_id=1, source_target_pairs={{0,1},{1,0},{2,3},{3,2},{4,5},{5,4},{6,7},{7,6},{8,9},{9,8},{10,11... | collective-permute-start | bytes 884744 | tf_op jit(solution)/shard_map/ppermute | solution.py:259
  31.3 8.5 %copy-start.4 = (f32[8,64]{1,0:T(8,128)S(1)}, f32[8,64]{1,0:T(8,128)}, u32[]{:S(2)}) copy-start(f32[8,64]{1,0:T(8,128)} %rest_13_.1) | copy-start | bytes 6148
  59.9 1.5 %collective-permute-start.9 = (bf16[8,2,8,8,128]{4,3,2,1,0:T(8,128)(2,1)S(1)}, bf16[8,2,8,8,128]{4,3,2,1,0:T(8,128)(2,1)S(1)}, u32[]{:S(2)}, u32[]{:S(2)}) collective-permute-start(bf16[8,2,8,8,128]{4,3,2,1,0:T(8,128)(2,1)S(1)} %bitcast.33), channel_id=1, source_target_pairs={{0,1},{1,0},{2,3},{3,2},{4,5},{5,4},{6,7},{7,6},{8,9},{9,8},{10,11... | collective-permute-start | bytes 786440 | tf_op jit(solution)/shard_map/ppermute | solution.py:259
  76.7 1.5 %collective-permute-start.10 = (bf16[8,2,8,8,128]{4,3,2,1,0:T(8,128)(2,1)S(1)}, bf16[8,2,8,8,128]{4,3,2,1,0:T(8,128)(2,1)S(1)}, u32[]{:S(2)}, u32[]{:S(2)}) collective-permute-start(bf16[8,2,8,8,128]{4,3,2,1,0:T(8,128)(2,1)S(1)} %bitcast.36), channel_id=1, source_target_pairs={{0,1},{1,0},{2,3},{3,2},{4,5},{5,4},{6,7},{7,6},{8,9},{9,8},{10,11... | collective-permute-start | bytes 786440 | tf_op jit(solution)/shard_map/ppermute | solution.py:259

commit v3 on v2

v3 whole, which is shorter than its diff:
```python
import functools

import jax
import jax.numpy as jnp
from jax import lax
from jax.experimental import pallas as pl
from jax.experimental.pallas import tpu as pltpu
from jax.sharding import Mesh, PartitionSpec as P


step_width = 0.05
highest = lax.Precision.HIGHEST
bf16 = jnp.bfloat16
f32 = jnp.float32
vmem = pl.BlockSpec(memory_space=pltpu.VMEM)
smem = pl.BlockSpec(memory_space=pltpu.SMEM)
hbm = pl.BlockSpec(memory_space=pltpu.HBM)
params = pltpu.CompilerParams(vmem_limit_bytes=32 * 2**20)


def local(x):
    return pltpu.with_memory_space_constraint(x, pltpu.VMEM)


def remote(x):
    return pltpu.with_memory_space_constraint(x, pltpu.HBM)


def pack_kernel(groups, place_ref, hist_hbm, *rest):
    out_refs, (hist_ref, wide_ref, turned_ref, sems) = rest[:-4], rest[-4:]
    rows = 128 * groups
    width = hist_ref.shape[1] // len(out_refs)
    half = width // 2
    chunks = [pl.ds(c * rows, rows) for c in range(hist_ref.shape[0] // rows)]
    copies = [
        pltpu.make_async_copy(hist_hbm.at[chunk], hist_ref.at[chunk], sems.at[c])
        for c, chunk in enumerate(chunks)
    ]
    for copy in copies:
        copy.start()
    for c, copy in enumerate(copies):
        copy.wait()
        wide_ref[chunks[c], :] = hist_ref[chunks[c], :].astype(f32)
        columns = slice(c * 128, (c + 1) * 128)
        for group in range(groups):
            turned = wide_ref[pl.ds(c * rows + group, 128, stride=groups), :].T
            for peer in range(len(out_refs)):
                turned_ref[group % 2, peer] = turned[peer * width : (peer + 1) * width]
            for offset, out_ref in enumerate(out_refs):
                for part in range(2):
                    start = (part * groups + group) * half
                    out_ref[start : start + half, columns] = turned_ref[
                        group % 2, place_ref[0] ^ offset, pl.ds(part, half, stride=2), :
                    ].astype(bf16)


def cubic_term(first_real, first_imag, other_real, other_imag):
    square_real = first_real * first_real - first_imag * first_imag
    square_imag = 2.0 * first_real * first_imag
    return (
        square_real * other_real + square_imag * other_imag,
        square_imag * other_real - square_real * other_imag,
    )


def energy_of(lesser, greater, weight_sq):
    half = lesser.shape[-1] // 2
    lr, li = lesser[:, :half], lesser[:, half:]
    gr, gi = greater[:, :half], greater[:, half:]
    less_real, less_imag = cubic_term(lr, li, gr, gi)
    more_real, more_imag = cubic_term(gr, gi, lr, li)
    return jnp.concatenate(
        [weight_sq * (more_real - less_real), weight_sq * (more_imag - less_imag)], axis=-1
    )


def send_energy(row_ref, coupling_ref, scratch_ref, send_ref):
    own_rows, slab, lanes = row_ref.shape
    for b in range(own_rows):
        row = row_ref[b]
        weight = coupling_ref[b : b + 1, :]
        scratch_ref[pl.ds(b, slab, stride=own_rows), :] = energy_of(
            row[:, : lanes // 2], row[:, lanes // 2 :], weight * weight
        )
    for t in range(slab):
        narrow = scratch_ref[t * own_rows : (t + 1) * own_rows, :].astype(bf16)
        for peer in range(send_ref.shape[0]):
            send_ref[peer, t] = narrow


def first_kernel(row_hbm, coupling_hbm, time_hbm, send_ref, row_ref, coupling_ref, time_ref, scratch_ref, sems):
    pairs = ((row_hbm, row_ref), (coupling_hbm, coupling_ref), (time_hbm, time_ref))
    copies = [pltpu.make_async_copy(a, b, sems.at[i]) for i, (a, b) in enumerate(pairs)]
    for copy in copies:
        copy.start()
    for copy in copies:
        copy.wait()
    slab, own_rows, lanes = row_ref.shape[1], row_ref.shape[0], send_ref.shape[3]
    send_energy(row_ref, coupling_ref, scratch_ref, send_ref)
    lane = lax.broadcasted_iota(jnp.int32, (own_rows, lanes), 1)
    times = jnp.zeros((own_rows, lanes), jnp.int32)
    for slot in range(time_ref.shape[0]):
        times = jnp.where(lane == slot, time_ref[slot], times)
    narrow = times.astype(f32).astype(bf16)
    for peer in range(send_ref.shape[0]):
        send_ref[peer, slab] = narrow


def build_kernel(pairs_ref, *out_refs):
    for w, out_ref in enumerate(out_refs):
        real, imag = pairs_ref[w, 0], pairs_ref[w, 1]
        size = real.shape[0]
        out_ref[:size, :] = jnp.concatenate([real, -imag], axis=1)
        out_ref[size:, :] = jnp.concatenate([imag, real], axis=1)


def energy_at(time, slab, place, core, own_ref, other_ref):
    inner = lax.rem(time, slab)
    group = lax.div(time, slab)
    far = lax.div(group, 2) ^ place
    same = lax.rem(group, 2) == core
    return [
        jnp.where(same, own_ref[peer, far, inner], other_ref[peer, far, inner])
        for peer in range(own_ref.shape[0])
    ]


def choose(time, alive, slab, place, core, own_ref, other_ref, chosen_ref, slot):
    own_rows = own_ref.shape[3]
    for peer, part in enumerate(energy_at(time, slab, place, core, own_ref, other_ref)):
        part = jnp.where(alive, part, jnp.zeros_like(part))
        chosen_ref[slot, peer * own_rows : (peer + 1) * own_rows, :] = part


def signs(lanes):
    return jnp.where(lax.broadcasted_iota(jnp.int32, (1, lanes), 1) < lanes // 2, -1.0, 1.0)


def combined(total):
    rows, lanes = total.shape
    return total[: rows // 2] + signs(lanes) * pltpu.roll(total[rows // 2 :], lanes // 2, 1)


def advance(sum_ref, row_ref, past_refs, columns, inverse_ref, out_ref):
    own_rows, slab, lanes = row_ref.shape
    lanes //= 2
    sign = signs(lanes)
    doubled = [
        jnp.concatenate(
            [c, (sign * pltpu.roll(c.astype(f32), lanes // 2, 1)).astype(bf16)], axis=0
        )
        for c in columns
    ]
    moved = []
    for m in range(2):
        integral = jnp.concatenate(
            [
                sum_ref[pl.ds(m * own_rows + b, slab, stride=2 * own_rows), :]
                for b in range(own_rows)
            ],
            axis=0,
        )
        for past_ref, column in zip(past_refs, doubled):
            past = past_ref[:, :, m * lanes : (m + 1) * lanes].reshape(own_rows * slab, lanes)
            high = past.astype(bf16)
            low = (past - high.astype(f32)).astype(bf16)
            integral += jnp.dot(high, column, preferred_element_type=f32)
            integral += jnp.dot(low, column, preferred_element_type=f32)
        row = row_ref[:, :, m * lanes : (m + 1) * lanes].reshape(own_rows * slab, lanes)
        moved.append(row + step_width * integral)
    moved = lax.dot_general(
        jnp.concatenate(moved, axis=0),
        inverse_ref[...],
        (((1,), (1,)), ((), ())),
        precision=highest,
        preferred_element_type=f32,
    )
    for m in range(2):
        out_ref[:, :, m * lanes : (m + 1) * lanes] = moved[
            m * own_rows * slab : (m + 1) * own_rows * slab
        ].reshape(own_rows, slab, lanes)


def step_kernel(peers, n_past, relative, last, scalar_ref, own_ref, other_ref, row_ref, *rest):
    hist_refs, rest = rest[:peers], rest[peers:]
    past_refs = rest[:n_past]
    inverse_ref, coupling_ref, out_ref = rest[n_past : n_past + 3]
    rest = rest[n_past + 3 :]
    if last:
        chosen_ref, sum_ref = rest
        send_ref = energy_ref = None
    else:
        send_ref, chosen_ref, sum_ref, energy_ref = rest
    slab = row_ref.shape[1]
    slots, orbitals, lanes = chosen_ref.shape
    block = slots // peers
    anchor, home, place, core = [scalar_ref[slots + i] for i in range(4)]
    place = place if relative else 0

    def select(source, slot):
        time = scalar_ref[(source ^ home) * block + slot]
        alive = time <= anchor
        to = source * block + slot
        choose(time, alive, slab, place, core, own_ref, other_ref, chosen_ref, to)

    if slots <= 32:
        for source in range(peers):
            for slot in range(block):
                select(source, slot)
    else:

        @pl.loop(0, peers)
        def _(source):
            for slot in range(block):
                select(source, slot)

    total = None
    for peer in range(peers):
        part = jnp.dot(
            hist_refs[peer][...],
            chosen_ref[peer * block : (peer + 1) * block].reshape(block * orbitals, lanes),
            preferred_element_type=f32,
        )
        total = part if total is None else total + part
    sum_ref[...] = combined(total)
    columns = []
    for past in range(n_past):
        choose(anchor + 1 + past, True, slab, place, core, own_ref, other_ref, chosen_ref, past)
        columns.append(chosen_ref[past])
    advance(sum_ref, row_ref, past_refs, columns, inverse_ref, out_ref)
    if not last:
        send_energy(out_ref, coupling_ref, energy_ref, send_ref)


def spread(block, axis):
    size = lax.axis_size(axis)
    gathered = block[None]
    stride = size // 2
    while stride:
        ring = [(i, i ^ stride) for i in range(size)]
        other = lax.ppermute(gathered, axis, ring)
        gathered = jnp.stack([gathered, other], axis=1).reshape(-1, *block.shape)
        stride //= 2
    return gathered


def body(history, row_now, coupling, step_inverse, start_step, history_time):
    slots_dev, orbitals, slab, parts, lanes = history.shape
    own_rows = row_now.shape[0]
    steps = step_inverse.shape[0]
    peers = lax.axis_size("hist")
    far = lax.axis_size("x")
    groups = slab * parts
    width = lanes // peers
    n_sum = groups * width
    rows = slab * own_rows
    swap = [(0, 1), (1, 0)]
    place = jnp.stack([lax.axis_index(name) for name in ("hist", "x", "c")])
    packed = pl.pallas_call(
        functools.partial(pack_kernel, groups),
        out_shape=[pltpu.VMEM((n_sum, slots_dev * orbitals), bf16)] * peers,
        in_specs=[smem, hbm],
        out_specs=[vmem] * peers,
        scratch_shapes=[
            pltpu.VMEM((slots_dev * orbitals * groups, lanes), bf16),
            pltpu.VMEM((slots_dev * orbitals * groups, lanes), f32),
            pltpu.VMEM((2, peers, width, 128), f32),
            pltpu.SemaphoreType.DMA((slots_dev * orbitals // 128,)),
        ],
        compiler_params=params,
        name="pack",
    )(place, remote(history.reshape(slots_dev * orbitals * groups, lanes)))
    sent = pl.pallas_call(
        first_kernel,
        out_shape=pltpu.VMEM((peers, slab + 1, own_rows, lanes), bf16),
        in_specs=[hbm] * 3,
        out_specs=vmem,
        scratch_shapes=[
            pltpu.VMEM(row_now.shape, f32),
            pltpu.VMEM(coupling.shape, f32),
            pltpu.SMEM((slots_dev,), jnp.int32),
            pltpu.VMEM((rows, lanes), f32),
            pltpu.SemaphoreType.DMA((3,)),
        ],
        compiler_params=params,
        name="first",
    )(remote(row_now), remote(coupling), remote(history_time))
    own = lax.all_to_all(sent, "hist", split_axis=0, concat_axis=0, tiled=True)
    times = own[:, slab, 0, :slots_dev].astype(jnp.int32).reshape(peers * slots_dev)
    scalars = jnp.concatenate([times, start_step, place])
    scalars = pltpu.with_memory_space_constraint(scalars, pltpu.SMEM)
    own = spread(own, "x").swapaxes(0, 1)
    moved = [packed[0]]
    for offset in range(1, peers):
        ring = [(i, i ^ offset) for i in range(peers)]
        moved.append(lax.ppermute(packed[offset], "hist", ring))
    inverse = pl.pallas_call(
        build_kernel,
        out_shape=[pltpu.VMEM((2 * orbitals, 2 * orbitals), f32)] * steps,
        in_specs=[vmem],
        out_specs=[vmem] * steps,
        compiler_params=params,
        name="build",
    )(step_inverse)
    green_shapes = [
        pltpu.VMEM(row_now.shape, f32),
        pltpu.VMEM((peers * far, slab, own_rows, lanes), bf16),
    ]
    green, past = row_now, []
    for w in range(steps):
        last = w == steps - 1
        if w:
            own = lax.all_to_all(sent, ("hist", "x"), split_axis=0, concat_axis=0, tiled=True)
            own = own.reshape(peers, far, slab, own_rows, lanes)
            past.append(green)
        other = lax.ppermute(own, "c", swap)
        outs = [jax.ShapeDtypeStruct(row_now.shape, f32)] if last else green_shapes
        scratch = [
            pltpu.VMEM((peers * slots_dev, orbitals, lanes), bf16),
            pltpu.VMEM((n_sum // 2, lanes), f32),
        ] + [pltpu.VMEM((rows, lanes), f32)] * (not last)
        result = pl.pallas_call(
            functools.partial(step_kernel, peers, len(past), w == 0, last),
            out_shape=outs,
            in_specs=[smem] + [vmem] * (5 + peers + len(past)),
            out_specs=[vmem] * len(outs),
            scratch_shapes=scratch,
            compiler_params=params,
        )(
            scalars,
            local(own),
            local(other),
            local(green),
            *[local(block) for block in moved],
            *[local(row) for row in past],
            local(inverse[w]),
            local(coupling),
        )
        green = result[0]
        if not last:
            sent = result[1]
    return green


def solution(mesh):
    n_hist, n_second = mesh.devices.shape
    split = Mesh(mesh.devices.reshape(n_hist, n_second // 2, 2), ("hist", "x", "c"))
    second = ("x", "c")
    placed = (
        P("hist", None, second, None, None),
        P("hist", second, None),
        P("hist", None),
        P(),
        P(),
        P("hist"),
    )
    return jax.shard_map(
        body, mesh=split, in_specs=placed, out_specs=P("hist", second, None), check_vma=False
    )
```

time: 80.9 us -> 88.2 us (1.090)
  blocking collectives: 31.8 us -> 46 us
  starting transfers between devices: 20.2 us -> 13.6 us
  local copies, waits for them, and re-layouts: 3.53 us -> 0.18 us
  waiting for transfers between devices: 14.9 us -> 17.7 us
    all_to_all x0 -> x1, blocking collectives: none -> 14.6 us  [body(): own = lax.all_to_all(sent, 'hist', split_axis=0, concat_axis=0, tiled=True)]
    all_to_all x1 -> x0, starting transfers between devices: 7.31 us -> none  [body(): own = lax.all_to_all(sent, 'hist', split_axis=0, concat_axis=0, tiled=True)]
    unnamed x14 -> x6, local copies, waits for them, and re-layouts: 3.42 us -> 0.01 us
    ppermute x7, waiting for transfers between devices: 8.37 us -> 10.9 us  [body(): moved.append(lax.ppermute(packed[offset], 'hist', ring))]
    pallas_call x5 -> x4, Pallas kernels: 5.87 us -> 5.91 us  [the longest x3 5.8 us: body(): pl.pallas_call(functools.partial(step_kernel, peers, len(past), w == 0, l...]
  transfers between devices with their start and end apart: 12 -> 11, of which waited for: 4 -> 8; matrix products, arithmetic and copies ran while one was open for 0% -> 0% of each run, Pallas kernels for 2% -> 3%
where the time goes in v3:
time: 88.2 us; the launch traced here: 87.9 us
  blocking collectives  46 us (52%)
  waiting for transfers between devices  17.7 us (20%)
  starting transfers between devices  13.6 us (15%)
  Pallas kernels  9.63 us (11%)
    all_to_all x2, blocking collectives, body(): lax.all_to_all(sent, ('hist', 'x'), split_axis=0, concat_axis=0, tiled=True)  31.4 us
    all_to_all x1, blocking collectives, body(): own = lax.all_to_all(sent, 'hist', split_axis=0, concat_axis=0, tiled=True)  14.6 us
    ppermute x7, starting transfers between devices, body(): moved.append(lax.ppermute(packed[offset], 'hist', ring))  12 us
    ppermute x7, waiting for transfers between devices, body(): moved.append(lax.ppermute(packed[offset], 'hist', ring))  10.9 us
    pallas_call x3, Pallas kernels, body(): pl.pallas_call(functools.partial(step_kernel, peers, len(past), w == 0, l...  5.8 us
    ppermute x1, waiting for transfers between devices, spread(): other = lax.ppermute(gathered, axis, ring)  3.65 us
    ppermute x3, waiting for transfers between devices, body(): other = lax.ppermute(own, 'c', swap)  3.07 us
    pallas_call x1, Pallas kernels, body(): pl.pallas_call(functools.partial(pack_kernel, groups), out_shape=[pltpu.V...  2.64 us
  transfers between devices with their start and end apart: 11, of which 8 were waited for; matrix products, arithmetic and copies ran while one was open for 0% of the time, Pallas kernels for 3%

profile of v3, /device:TPU:0, one launch (start us, length us, event | category | flops | bytes accessed | tf_op | source)
XLA Modules:
  0.0 87.9 jit_solution(6334411714974087049)
XLA Ops:
  0.0 1.1 %first.1 = bf16[8,9,8,128]{3,2,1,0:T(8,128)(2,1)S(1)} custom-call(f32[8,8,256]{2,1,0:T(8,128)} %row_ref.1, f32[8,64]{1,0:T(8,128)} %rest_11_.1, s32[4]{0:T(128)} %time_hbm.1), custom_call_target="tpu_custom_call" | custom-call | tf_op jit(solution)/shard_map/first/pallas_call | solution.py:273
  1.1 14.6 %all_to_all.15 = bf16[8,9,8,128]{3,2,1,0:T(8,128)(2,1)S(1)} all-to-all(bf16[8,9,8,128]{3,2,1,0:T(8,128)(2,1)S(1)} %first.1), channel_id=1, replica_groups=mesh['hist'=8,'x'=2,'c'=2] {'hist'}, dimensions={0} | all-to-all | bytes 294912 | tf_op jit(solution)/shard_map/all_to_all | solution.py:288
  15.6 1.5 %collective-permute-start = (bf16[1,8,9,8,128]{4,3,2,1,0:T(8,128)(2,1)S(1)}, bf16[1,8,9,8,128]{4,3,2,1,0:T(8,128)(2,1)S(1)}, u32[]{:S(2)}, u32[]{:S(2)}) collective-permute-start(bf16[1,8,9,8,128]{4,3,2,1,0:T(8,128)(2,1)S(1)} %bitcast.20), channel_id=1, source_target_pairs={{0,2},{2,0},{1,3},{3,1},{4,6},{6,4},{5,7},{7,5},{8,10},{10,8},{9,1... | collective-permute-start | bytes 442376 | tf_op jit(solution)/shard_map/ppermute | solution.py:241
  17.1 3.7 %collective-permute-done = bf16[1,8,9,8,128]{4,3,2,1,0:T(8,128)(2,1)S(1)} collective-permute-done((bf16[1,8,9,8,128]{4,3,2,1,0:T(8,128)(2,1)S(1)}, bf16[1,8,9,8,128]{4,3,2,1,0:T(8,128)(2,1)S(1)}, u32[]{:S(2)}, u32[]{:S(2)}) %collective-permute-start) | collective-permute-done | bytes 147488 | tf_op jit(solution)/shard_map/ppermute | solution.py:241
  21.0 2.6 %pack.1 = (bf16[256,256]{1,0:T(8,128)(2,1)S(1)}, bf16[256,256]{1,0:T(8,128)(2,1)S(1)}, bf16[256,256]{1,0:T(8,128)(2,1)S(1)}, bf16[256,256]{1,0:T(8,128)(2,1)S(1)...) custom-call(s32[3]{0:T(128)S(1)} %pad_add_fusion.place_ref, ...), custom_call_target="tpu_custom_call" | custom-call | tf_op jit(solution)/shard_map/pack/pallas_call | solution.py:259
  23.6 0.4 collective-permute-start.2
  24.0 1.0 %collective-permute-start.3 = (bf16[256,256]{1,0:T(8,128)(2,1)S(1)}, bf16[256,256]{1,0:T(8,128)(2,1)S(1)}, u32[]{:S(2)}, u32[]{:S(2)}) collective-permute-start(bf16[256,256]{1,0:T(8,128)(2,1)S(1)} %get-tuple-element.22), channel_id=1, source_target_pairs={{0,8},{4,12},{8,0},{12,4},{16,24},{20,28},{24,16},{28,20},{1,9},{5... | collective-permute-start | bytes 393224 | tf_op jit(solution)/shard_map/ppermute | solution.py:296
  25.0 2.2 %collective-permute-start.4 = (bf16[256,256]{1,0:T(8,128)(2,1)S(1)}, bf16[256,256]{1,0:T(8,128)(2,1)S(1)}, u32[]{:S(2)}, u32[]{:S(2)}) collective-permute-start(bf16[256,256]{1,0:T(8,128)(2,1)S(1)} %get-tuple-element.23), channel_id=1, source_target_pairs={{0,12},{4,8},{8,4},{12,0},{16,28},{20,24},{24,20},{28,16},{1,13},{... | collective-permute-start | bytes 393224 | tf_op jit(solution)/shard_map/ppermute | solution.py:296
  27.2 0.4 collective-permute-start.5
  27.6 2.0 %collective-permute-done.2.rest_1_ = bf16[256,256]{1,0:T(8,128)(2,1)S(1)} collective-permute-done((bf16[256,256]{1,0:T(8,128)(2,1)S(1)}, bf16[256,256]{1,0:T(8,128)(2,1)S(1)}, u32[]{:S(2)}, u32[]{:S(2)}) %collective-permute-start.2) | collective-permute-done | bytes 131104 | tf_op jit(solution)/shard_map/ppermute | solution.py:296
  29.6 0.3 collective-permute-start.6
  29.9 0.5 collective-permute-done.3.rest_2_
  30.4 5.5 %collective-permute-start.7 = (bf16[256,256]{1,0:T(8,128)(2,1)S(1)}, bf16[256,256]{1,0:T(8,128)(2,1)S(1)}, u32[]{:S(2)}, u32[]{:S(2)}) collective-permute-start(bf16[256,256]{1,0:T(8,128)(2,1)S(1)} %get-tuple-element.26), channel_id=1, source_target_pairs={{0,24},{4,28},{8,16},{12,20},{16,8},{20,12},{24,0},{28,4},{1,25},{... | collective-permute-start | bytes 393224 | tf_op jit(solution)/shard_map/ppermute | solution.py:296
  35.9 0.9 collective-permute-done.4.rest_3_
  36.8 2.2 %collective-permute-start.8 = (bf16[256,256]{1,0:T(8,128)(2,1)S(1)}, bf16[256,256]{1,0:T(8,128)(2,1)S(1)}, u32[]{:S(2)}, u32[]{:S(2)}) collective-permute-start(bf16[256,256]{1,0:T(8,128)(2,1)S(1)} %get-tuple-element.27), channel_id=1, source_target_pairs={{0,28},{4,24},{8,20},{12,16},{16,12},{20,8},{24,4},{28,0},{1,29},{... | collective-permute-start | bytes 393224 | tf_op jit(solution)/shard_map/ppermute | solution.py:296
  40.0 5.5 %collective-permute-done.5.rest_4_ = bf16[256,256]{1,0:T(8,128)(2,1)S(1)} collective-permute-done((bf16[256,256]{1,0:T(8,128)(2,1)S(1)}, bf16[256,256]{1,0:T(8,128)(2,1)S(1)}, u32[]{:S(2)}, u32[]{:S(2)}) %collective-permute-start.5) | collective-permute-done | bytes 131104 | tf_op jit(solution)/shard_map/ppermute | solution.py:296
  45.5 2.1 %collective-permute-done.6.rest_5_ = bf16[256,256]{1,0:T(8,128)(2,1)S(1)} collective-permute-done((bf16[256,256]{1,0:T(8,128)(2,1)S(1)}, bf16[256,256]{1,0:T(8,128)(2,1)S(1)}, u32[]{:S(2)}, u32[]{:S(2)}) %collective-permute-start.6) | collective-permute-done | bytes 131104 | tf_op jit(solution)/shard_map/ppermute | solution.py:296
  47.6 1.7 %shard_map.64 = (f32[8,8,256]{2,1,0:T(8,128)S(1)}, bf16[16,8,8,128]{3,2,1,0:T(8,128)(2,1)S(1)}) custom-call(s32[36]{0:T(128)S(1)} %concatenate.4.scalar_ref, bf16[8,2,9,8,128]{4,3,2,1,0:T(8,128)(2,1)S(1)} %maximum_bitcast_fusion.own_ref, bf16[8,2,9,8,128]{4,3,2,1,0:T(8,128)(2,1)S(1)} %collective-permute-done.1.other_ref, f32[8,8,256]{2,1,0:T(8,128)S(1)} %copy-done, ...), custom_call_target="tpu_custom_call" | custom-call | tf_op jit(solution)/shard_map/pallas_call | solution.py:322
  49.4 17.9 %all_to_all.16 = bf16[16,8,8,128]{3,2,1,0:T(8,128)(2,1)S(1)} all-to-all(bf16[16,8,8,128]{3,2,1,0:T(8,128)(2,1)S(1)} %get-tuple-element.29), channel_id=1, replica_groups=mesh['hist'=8,'x'=2,'c'=2] {'hist','x'}, dimensions={0} | all-to-all | bytes 524288 | tf_op jit(solution)/shard_map/all_to_all | solution.py:313
  67.3 1.5 %collective-permute-done.9.other_ref = bf16[8,2,8,8,128]{4,3,2,1,0:T(8,128)(2,1)S(1)} collective-permute-done((bf16[8,2,8,8,128]{4,3,2,1,0:T(8,128)(2,1)S(1)}, bf16[8,2,8,8,128]{4,3,2,1,0:T(8,128)(2,1)S(1)}, u32[]{:S(2)}, u32[]{:S(2)}) %collective-permute-start.9) | collective-permute-done | bytes 262176 | tf_op jit(solution)/shard_map/ppermute | solution.py:316
  68.8 1.8 %shard_map.65 = (f32[8,8,256]{2,1,0:T(8,128)S(1)}, bf16[16,8,8,128]{3,2,1,0:T(8,128)(2,1)S(1)}) custom-call(s32[36]{0:T(128)S(1)} %concatenate.4.scalar_ref, bf16[8,2,8,8,128]{4,3,2,1,0:T(8,128)(2,1)S(1)} %bitcast.18, bf16[8,2,8,8,128]{4,3,2,1,0:T(8,128)(2,1)S(1)} %collective-permute-done.9.other_ref, f32[8,8,256]{2,1,0:T(8,128)S(1)} %get-tuple-element.30.row_ref.rest_8_, ...), custom_call_target="tpu_custom_call" | custom-call | tf_op jit(solution)/shard_map/pallas_call | solution.py:322
  70.6 13.5 %all_to_all.17 = bf16[16,8,8,128]{3,2,1,0:T(8,128)(2,1)S(1)} all-to-all(bf16[16,8,8,128]{3,2,1,0:T(8,128)(2,1)S(1)} %get-tuple-element.32), channel_id=1, replica_groups=mesh['hist'=8,'x'=2,'c'=2] {'hist','x'}, dimensions={0} | all-to-all | bytes 524288 | tf_op jit(solution)/shard_map/all_to_all | solution.py:313
  84.1 1.5 %collective-permute-done.10.other_ref = bf16[8,2,8,8,128]{4,3,2,1,0:T(8,128)(2,1)S(1)} collective-permute-done((bf16[8,2,8,8,128]{4,3,2,1,0:T(8,128)(2,1)S(1)}, bf16[8,2,8,8,128]{4,3,2,1,0:T(8,128)(2,1)S(1)}, u32[]{:S(2)}, u32[]{:S(2)}) %collective-permute-start.10) | collective-permute-done | bytes 262176 | tf_op jit(solution)/shard_map/ppermute | solution.py:316
  85.7 2.2 %shard_map.66 = f32[8,8,256]{2,1,0:T(8,128)} custom-call(s32[36]{0:T(128)S(1)} %concatenate.4.scalar_ref, bf16[8,2,8,8,128]{4,3,2,1,0:T(8,128)(2,1)S(1)} %bitcast.16, bf16[8,2,8,8,128]{4,3,2,1,0:T(8,128)(2,1)S(1)} %collective-permute-done.10.other_ref, f32[8,8,256]{2,1,0:T(8,128)S(1)} %get-tuple-element.33.row_ref.rest_9_, ...), custom_call_target="tpu_custom_call" | custom-call | tf_op jit(solution)/shard_map/pallas_call | solution.py:322
  (18 shorter events, 0.5 us)
Async XLA Ops:
  15.6 5.1 %collective-permute-start = (bf16[1,8,9,8,128]{4,3,2,1,0:T(8,128)(2,1)S(1)}, bf16[1,8,9,8,128]{4,3,2,1,0:T(8,128)(2,1)S(1)}, u32[]{:S(2)}, u32[]{:S(2)}) collective-permute-start(bf16[1,8,9,8,128]{4,3,2,1,0:T(8,128)(2,1)S(1)} %bitcast.20), channel_id=1, source_target_pairs={{0,2},{2,0},{1,3},{3,1},{4,6},{6,4},{5,7},{7,5},{8,10},{10,8},{9,1... | collective-permute-start | bytes 442376 | tf_op jit(solution)/shard_map/ppermute | solution.py:241
  20.8 26.8 %collective-permute-start.1 = (bf16[8,2,9,8,128]{4,3,2,1,0:T(8,128)(2,1)S(1)}, bf16[8,2,9,8,128]{4,3,2,1,0:T(8,128)(2,1)S(1)}, u32[]{:S(2)}, u32[]{:S(2)}) collective-permute-start(bf16[8,2,9,8,128]{4,3,2,1,0:T(8,128)(2,1)S(1)} %maximum_bitcast_fusion.own_ref), channel_id=1, source_target_pairs={{0,1},{1,0},{2,3},{3,2},{4,5},{5,4},{6,7},{7,6},{8,9},{9,8},{10,11... | collective-permute-start | bytes 884744 | tf_op jit(solution)/shard_map/ppermute | solution.py:316
  21.0 18.7 %copy-start.1 = (f32[3,2,64,64]{3,2,1,0:T(8,128)S(1)}, f32[3,2,64,64]{3,2,1,0:T(8,128)}, u32[]{:S(2)}) copy-start(f32[3,2,64,64]{3,2,1,0:T(8,128)} %pairs_ref.1) | copy-start | bytes 294916
  23.6 6.0 %collective-permute-start.2 = (bf16[256,256]{1,0:T(8,128)(2,1)S(1)}, bf16[256,256]{1,0:T(8,128)(2,1)S(1)}, u32[]{:S(2)}, u32[]{:S(2)}) collective-permute-start(bf16[256,256]{1,0:T(8,128)(2,1)S(1)} %get-tuple-element.21), channel_id=1, source_target_pairs={{0,4},{4,0},{8,12},{12,8},{16,20},{20,16},{24,28},{28,24},{1,5},{5... | collective-permute-start | bytes 393224 | tf_op jit(solution)/shard_map/ppermute | solution.py:296
  24.0 6.4 %collective-permute-start.3 = (bf16[256,256]{1,0:T(8,128)(2,1)S(1)}, bf16[256,256]{1,0:T(8,128)(2,1)S(1)}, u32[]{:S(2)}, u32[]{:S(2)}) collective-permute-start(bf16[256,256]{1,0:T(8,128)(2,1)S(1)} %get-tuple-element.22), channel_id=1, source_target_pairs={{0,8},{4,12},{8,0},{12,4},{16,24},{20,28},{24,16},{28,20},{1,9},{5... | collective-permute-start | bytes 393224 | tf_op jit(solution)/shard_map/ppermute | solution.py:296
  25.0 11.8 %collective-permute-start.4 = (bf16[256,256]{1,0:T(8,128)(2,1)S(1)}, bf16[256,256]{1,0:T(8,128)(2,1)S(1)}, u32[]{:S(2)}, u32[]{:S(2)}) collective-permute-start(bf16[256,256]{1,0:T(8,128)(2,1)S(1)} %get-tuple-element.23), channel_id=1, source_target_pairs={{0,12},{4,8},{8,4},{12,0},{16,28},{20,24},{24,20},{28,16},{1,13},{... | collective-permute-start | bytes 393224 | tf_op jit(solution)/shard_map/ppermute | solution.py:296
  27.2 18.3 %collective-permute-start.5 = (bf16[256,256]{1,0:T(8,128)(2,1)S(1)}, bf16[256,256]{1,0:T(8,128)(2,1)S(1)}, u32[]{:S(2)}, u32[]{:S(2)}) collective-permute-start(bf16[256,256]{1,0:T(8,128)(2,1)S(1)} %get-tuple-element.24), channel_id=1, source_target_pairs={{0,16},{4,20},{8,24},{12,28},{16,0},{20,4},{24,8},{28,12},{1,17},{... | collective-permute-start | bytes 393224 | tf_op jit(solution)/shard_map/ppermute | solution.py:296
  29.6 18.0 %collective-permute-start.6 = (bf16[256,256]{1,0:T(8,128)(2,1)S(1)}, bf16[256,256]{1,0:T(8,128)(2,1)S(1)}, u32[]{:S(2)}, u32[]{:S(2)}) collective-permute-start(bf16[256,256]{1,0:T(8,128)(2,1)S(1)} %get-tuple-element.25), channel_id=1, source_target_pairs={{0,20},{4,16},{8,28},{12,24},{16,4},{20,0},{24,12},{28,8},{1,21},{... | collective-permute-start | bytes 393224 | tf_op jit(solution)/shard_map/ppermute | solution.py:296
  30.4 17.2 %collective-permute-start.7 = (bf16[256,256]{1,0:T(8,128)(2,1)S(1)}, bf16[256,256]{1,0:T(8,128)(2,1)S(1)}, u32[]{:S(2)}, u32[]{:S(2)}) collective-permute-start(bf16[256,256]{1,0:T(8,128)(2,1)S(1)} %get-tuple-element.26), channel_id=1, source_target_pairs={{0,24},{4,28},{8,16},{12,20},{16,8},{20,12},{24,0},{28,4},{1,25},{... | collective-permute-start | bytes 393224 | tf_op jit(solution)/shard_map/ppermute | solution.py:296
  36.8 10.8 %collective-permute-start.8 = (bf16[256,256]{1,0:T(8,128)(2,1)S(1)}, bf16[256,256]{1,0:T(8,128)(2,1)S(1)}, u32[]{:S(2)}, u32[]{:S(2)}) collective-permute-start(bf16[256,256]{1,0:T(8,128)(2,1)S(1)} %get-tuple-element.27), channel_id=1, source_target_pairs={{0,28},{4,24},{8,20},{12,16},{16,12},{20,8},{24,4},{28,0},{1,29},{... | collective-permute-start | bytes 393224 | tf_op jit(solution)/shard_map/ppermute | solution.py:296
  39.7 7.9 %copy-start = (f32[8,8,256]{2,1,0:T(8,128)S(1)}, f32[8,8,256]{2,1,0:T(8,128)}, u32[]{:S(2)}) copy-start(f32[8,8,256]{2,1,0:T(8,128)} %row_ref.1) | copy-start | bytes 196612
  39.9 7.7 %copy-start.2 = (f32[8,64]{1,0:T(8,128)S(1)}, f32[8,64]{1,0:T(8,128)}, u32[]{:S(2)}) copy-start(f32[8,64]{1,0:T(8,128)} %rest_11_.1) | copy-start | bytes 6148
  67.3 1.5 %collective-permute-start.9 = (bf16[8,2,8,8,128]{4,3,2,1,0:T(8,128)(2,1)S(1)}, bf16[8,2,8,8,128]{4,3,2,1,0:T(8,128)(2,1)S(1)}, u32[]{:S(2)}, u32[]{:S(2)}) collective-permute-start(bf16[8,2,8,8,128]{4,3,2,1,0:T(8,128)(2,1)S(1)} %bitcast.17), channel_id=1, source_target_pairs={{0,1},{1,0},{2,3},{3,2},{4,5},{5,4},{6,7},{7,6},{8,9},{9,8},{10,11... | collective-permute-start | bytes 786440 | tf_op jit(solution)/shard_map/ppermute | solution.py:316
  84.1 1.5 %collective-permute-start.10 = (bf16[8,2,8,8,128]{4,3,2,1,0:T(8,128)(2,1)S(1)}, bf16[8,2,8,8,128]{4,3,2,1,0:T(8,128)(2,1)S(1)}, u32[]{:S(2)}, u32[]{:S(2)}) collective-permute-start(bf16[8,2,8,8,128]{4,3,2,1,0:T(8,128)(2,1)S(1)} %bitcast.15), channel_id=1, source_target_pairs={{0,1},{1,0},{2,3},{3,2},{4,5},{5,4},{6,7},{7,6},{8,9},{9,8},{10,11... | collective-permute-start | bytes 786440 | tf_op jit(solution)/shard_map/ppermute | solution.py:316

commit v4 on v3

--- a/solution.py
+++ b/solution.py
@@ -43,7 +43,8 @@
         wide_ref[chunks[c], :] = hist_ref[chunks[c], :].astype(f32)
         columns = slice(c * 128, (c + 1) * 128)
         for group in range(groups):
-            turned = wide_ref[pl.ds(c * rows + group, 128, stride=groups), :].T
+            tile = wide_ref[pl.ds(c * rows + group, 128, stride=groups), :]
+            turned = tile.astype(bf16).T.astype(f32)
             for peer in range(len(out_refs)):
                 turned_ref[group % 2, peer] = turned[peer * width : (peer + 1) * width]
             for offset, out_ref in enumerate(out_refs):
@@ -125,13 +126,6 @@
     ]
 
 
-def choose(time, alive, slab, place, core, own_ref, other_ref, chosen_ref, slot):
-    own_rows = own_ref.shape[3]
-    for peer, part in enumerate(energy_at(time, slab, place, core, own_ref, other_ref)):
-        part = jnp.where(alive, part, jnp.zeros_like(part))
-        chosen_ref[slot, peer * own_rows : (peer + 1) * own_rows, :] = part
-
-
 def signs(lanes):
     return jnp.where(lax.broadcasted_iota(jnp.int32, (1, lanes), 1) < lanes // 2, -1.0, 1.0)
 
@@ -191,28 +185,33 @@
         send_ref = energy_ref = None
     else:
         send_ref, chosen_ref, sum_ref, energy_ref = rest
-    slab = row_ref.shape[1]
+    own_rows, slab = row_ref.shape[:2]
     slots, orbitals, lanes = chosen_ref.shape
     block = slots // peers
-    anchor, home, place, core = [scalar_ref[slots + i] for i in range(4)]
+    anchor, place, core = [scalar_ref[slots + i] for i in (0, 2, 3)]
     place = place if relative else 0
 
-    def select(source, slot):
-        time = scalar_ref[(source ^ home) * block + slot]
+    def select(far, side, inner):
+        time = ((far ^ place) * 2 + (core ^ side)) * slab + inner
+        slot = scalar_ref[time]
         alive = time <= anchor
-        to = source * block + slot
-        choose(time, alive, slab, place, core, own_ref, other_ref, chosen_ref, to)
+        source_ref = other_ref if side else own_ref
+        for peer in range(peers):
+            part = source_ref[peer, far, inner]
+            chosen_ref[slot, peer * own_rows : (peer + 1) * own_rows, :] = jnp.where(
+                alive, part, jnp.zeros_like(part)
+            )
+
+    def select_all(inner):
+        for far in range(own_ref.shape[1]):
+            for side in range(2):
+                select(far, side, inner)
 
     if slots <= 32:
-        for source in range(peers):
-            for slot in range(block):
-                select(source, slot)
+        for inner in range(slab):
+            select_all(inner)
     else:
-
-        @pl.loop(0, peers)
-        def _(source):
-            for slot in range(block):
-                select(source, slot)
+        pl.loop(0, slab)(select_all)
 
     total = None
     for peer in range(peers):
@@ -225,7 +224,9 @@
     sum_ref[...] = combined(total)
     columns = []
     for past in range(n_past):
-        choose(anchor + 1 + past, True, slab, place, core, own_ref, other_ref, chosen_ref, past)
+        parts = energy_at(anchor + 1 + past, slab, place, core, own_ref, other_ref)
+        for peer, part in enumerate(parts):
+            chosen_ref[past, peer * own_rows : (peer + 1) * own_rows, :] = part
         columns.append(chosen_ref[past])
     advance(sum_ref, row_ref, past_refs, columns, inverse_ref, out_ref)
     if not last:
@@ -287,7 +288,10 @@
     )(remote(row_now), remote(coupling), remote(history_time))
     own = lax.all_to_all(sent, "hist", split_axis=0, concat_axis=0, tiled=True)
     times = own[:, slab, 0, :slots_dev].astype(jnp.int32).reshape(peers * slots_dev)
-    scalars = jnp.concatenate([times, start_step, place])
+    source = (jnp.arange(peers) ^ place[0])[:, None] * slots_dev + jnp.arange(slots_dev)[None, :]
+    found = times[None, :] == jnp.arange(peers * slots_dev)[:, None]
+    slot_of = jnp.sum(jnp.where(found, source.reshape(1, -1), 0), axis=1, dtype=jnp.int32)
+    scalars = jnp.concatenate([slot_of, start_step, place])
     scalars = pltpu.with_memory_space_constraint(scalars, pltpu.SMEM)
     own = spread(own, "x").swapaxes(0, 1)
     moved = [packed[0]]

time: 88.2 us -> 84.2 us (0.955)
  blocking collectives: 46 us -> 31.9 us
  starting transfers between devices: 13.6 us -> 19 us
  waiting for transfers between devices: 17.7 us -> 21.3 us
    all_to_all x1 -> x0, blocking collectives: 14.6 us -> none  [body(): own = lax.all_to_all(sent, 'hist', split_axis=0, concat_axis=0, tiled=True)]
    all_to_all x0 -> x1, waiting for transfers between devices: none -> 7.45 us  [body(): own = lax.all_to_all(sent, 'hist', split_axis=0, concat_axis=0, tiled=True)]
    all_to_all x0 -> x1, starting transfers between devices: none -> 7.32 us  [body(): own = lax.all_to_all(sent, 'hist', split_axis=0, concat_axis=0, tiled=True)]
    ppermute x1, waiting for transfers between devices: 3.65 us -> 0.01 us  [spread(): other = lax.ppermute(gathered, axis, ring)]
    ppermute x7, starting transfers between devices: 12 us -> 10.2 us  [body(): moved.append(lax.ppermute(packed[offset], 'hist', ring))]
  transfers between devices with their start and end apart: 11 -> 12, of which waited for: 8 -> 7; matrix products, arithmetic and copies ran while one was open for 0% -> 1% of each run, Pallas kernels for 3% -> 3%
where the time goes in v4:
time: 84.2 us; the launch traced here: 83.8 us
  blocking collectives  31.9 us (38%)
  waiting for transfers between devices  21.3 us (25%)
  starting transfers between devices  19 us (23%)
  Pallas kernels  10.2 us (12%)
    all_to_all x2, blocking collectives, body(): lax.all_to_all(sent, ('hist', 'x'), split_axis=0, concat_axis=0, tiled=True)  31.9 us
    ppermute x7, waiting for transfers between devices, body(): moved.append(lax.ppermute(packed[offset], 'hist', ring))  10.8 us
    ppermute x7, starting transfers between devices, body(): moved.append(lax.ppermute(packed[offset], 'hist', ring))  10.2 us
    all_to_all x1, waiting for transfers between devices, body(): own = lax.all_to_all(sent, 'hist', split_axis=0, concat_axis=0, tiled=True)  7.45 us
    all_to_all x1, starting transfers between devices, body(): own = lax.all_to_all(sent, 'hist', split_axis=0, concat_axis=0, tiled=True)  7.32 us
    pallas_call x3, Pallas kernels, body(): pl.pallas_call(functools.partial(step_kernel, peers, len(past), w == 0, l...  5.78 us
    ppermute x3, waiting for transfers between devices, body(): other = lax.ppermute(own, 'c', swap)  3.07 us
    pallas_call x1, Pallas kernels, body(): pl.pallas_call(functools.partial(pack_kernel, groups), out_shape=[pltpu.V...  2.6 us
  transfers between devices with their start and end apart: 12, of which 7 were waited for; matrix products, arithmetic and copies ran while one was open for 1% of the time, Pallas kernels for 3%

profile of v4, /device:TPU:0, one launch (start us, length us, event | category | flops | bytes accessed | tf_op | source)
XLA Modules:
  0.0 83.8 jit_solution(5783531856312403550)
XLA Ops:
  0.0 1.7 %first.1 = bf16[8,9,8,128]{3,2,1,0:T(8,128)(2,1)} custom-call(f32[8,8,256]{2,1,0:T(8,128)} %row_ref.1, f32[8,64]{1,0:T(8,128)} %rest_11_.1, s32[4]{0:T(128)} %time_hbm.1), custom_call_target="tpu_custom_call" | custom-call | tf_op jit(solution)/shard_map/first/pallas_call | solution.py:274
  1.7 7.3 %all-to-all-start = ((bf16[8,9,8,128]{3,2,1,0:T(8,128)(2,1)}), bf16[8,9,8,128]{3,2,1,0:T(8,128)(2,1)S(1)}, u32[]{:S(2)}, u32[]{:S(2)}) async-start(bf16[8,9,8,128]{3,2,1,0:T(8,128)(2,1)} %first.1), calls=%async_computation | async-start | bytes 294912 | tf_op jit(solution)/shard_map/all_to_all | solution.py:289
  9.1 7.5 %all-to-all-done = bf16[8,9,8,128]{3,2,1,0:T(8,128)(2,1)S(1)} async-done(((bf16[8,9,8,128]{3,2,1,0:T(8,128)(2,1)}), bf16[8,9,8,128]{3,2,1,0:T(8,128)(2,1)S(1)}, u32[]{:S(2)}, u32[]{:S(2)}) %all-to-all-start) | async-done | bytes 147488 | tf_op jit(solution)/shard_map/all_to_all | solution.py:289
  16.5 1.5 %collective-permute-start = (bf16[1,8,9,8,128]{4,3,2,1,0:T(8,128)(2,1)S(1)}, bf16[1,8,9,8,128]{4,3,2,1,0:T(8,128)(2,1)S(1)}, u32[]{:S(2)}, u32[]{:S(2)}) collective-permute-start(bf16[1,8,9,8,128]{4,3,2,1,0:T(8,128)(2,1)S(1)} %bitcast.20), channel_id=1, source_target_pairs={{0,2},{2,0},{1,3},{3,1},{4,6},{6,4},{5,7},{7,5},{8,10},{10,8},{9,1... | collective-permute-start | bytes 442376 | tf_op jit(solution)/shard_map/ppermute | solution.py:242
  18.1 2.6 %pack.1 = (bf16[256,256]{1,0:T(8,128)(2,1)S(1)}, bf16[256,256]{1,0:T(8,128)(2,1)S(1)}, bf16[256,256]{1,0:T(8,128)(2,1)S(1)}, bf16[256,256]{1,0:T(8,128)(2,1)S(1)...) custom-call(s32[3]{0:T(128)S(1)} %pad_add_fusion.place_ref, ...), custom_call_target="tpu_custom_call" | custom-call | tf_op jit(solution)/shard_map/pack/pallas_call | solution.py:260
  20.7 0.4 collective-permute-start.2
  21.1 1.0 %collective-permute-start.3 = (bf16[256,256]{1,0:T(8,128)(2,1)S(1)}, bf16[256,256]{1,0:T(8,128)(2,1)S(1)}, u32[]{:S(2)}, u32[]{:S(2)}) collective-permute-start(bf16[256,256]{1,0:T(8,128)(2,1)S(1)} %get-tuple-element.22), channel_id=1, source_target_pairs={{0,8},{4,12},{8,0},{12,4},{16,24},{20,28},{24,16},{28,20},{1,9},{5... | collective-permute-start | bytes 393224 | tf_op jit(solution)/shard_map/ppermute | solution.py:300
  22.1 2.1 %collective-permute-start.4 = (bf16[256,256]{1,0:T(8,128)(2,1)S(1)}, bf16[256,256]{1,0:T(8,128)(2,1)S(1)}, u32[]{:S(2)}, u32[]{:S(2)}) collective-permute-start(bf16[256,256]{1,0:T(8,128)(2,1)S(1)} %get-tuple-element.23), channel_id=1, source_target_pairs={{0,12},{4,8},{8,4},{12,0},{16,28},{20,24},{24,20},{28,16},{1,13},{... | collective-permute-start | bytes 393224 | tf_op jit(solution)/shard_map/ppermute | solution.py:300
  24.2 0.4 collective-permute-start.5
  25.6 0.1 build.1
  25.7 0.6 collective-permute-done.2.rest_1_
  26.3 1.8 %collective-permute-start.6 = (bf16[256,256]{1,0:T(8,128)(2,1)S(1)}, bf16[256,256]{1,0:T(8,128)(2,1)S(1)}, u32[]{:S(2)}, u32[]{:S(2)}) collective-permute-start(bf16[256,256]{1,0:T(8,128)(2,1)S(1)} %get-tuple-element.25), channel_id=1, source_target_pairs={{0,20},{4,16},{8,28},{12,24},{16,4},{20,0},{24,12},{28,8},{1,21},{... | collective-permute-start | bytes 393224 | tf_op jit(solution)/shard_map/ppermute | solution.py:300
  28.1 2.2 %collective-permute-start.7 = (bf16[256,256]{1,0:T(8,128)(2,1)S(1)}, bf16[256,256]{1,0:T(8,128)(2,1)S(1)}, u32[]{:S(2)}, u32[]{:S(2)}) collective-permute-start(bf16[256,256]{1,0:T(8,128)(2,1)S(1)} %get-tuple-element.26), channel_id=1, source_target_pairs={{0,24},{4,28},{8,16},{12,20},{16,8},{20,12},{24,0},{28,4},{1,25},{... | collective-permute-start | bytes 393224 | tf_op jit(solution)/shard_map/ppermute | solution.py:300
  30.3 0.9 %collective-permute-done.4.rest_3_ = bf16[256,256]{1,0:T(8,128)(2,1)S(1)} collective-permute-done((bf16[256,256]{1,0:T(8,128)(2,1)S(1)}, bf16[256,256]{1,0:T(8,128)(2,1)S(1)}, u32[]{:S(2)}, u32[]{:S(2)}) %collective-permute-start.4) | collective-permute-done | bytes 131104 | tf_op jit(solution)/shard_map/ppermute | solution.py:300
  31.1 2.2 %collective-permute-start.8 = (bf16[256,256]{1,0:T(8,128)(2,1)S(1)}, bf16[256,256]{1,0:T(8,128)(2,1)S(1)}, u32[]{:S(2)}, u32[]{:S(2)}) collective-permute-start(bf16[256,256]{1,0:T(8,128)(2,1)S(1)} %get-tuple-element.27), channel_id=1, source_target_pairs={{0,28},{4,24},{8,20},{12,16},{16,12},{20,8},{24,4},{28,0},{1,29},{... | collective-permute-start | bytes 393224 | tf_op jit(solution)/shard_map/ppermute | solution.py:300
  33.6 7.1 %collective-permute-done.5.rest_4_ = bf16[256,256]{1,0:T(8,128)(2,1)S(1)} collective-permute-done((bf16[256,256]{1,0:T(8,128)(2,1)S(1)}, bf16[256,256]{1,0:T(8,128)(2,1)S(1)}, u32[]{:S(2)}, u32[]{:S(2)}) %collective-permute-start.5) | collective-permute-done | bytes 131104 | tf_op jit(solution)/shard_map/ppermute | solution.py:300
  40.7 2.3 %collective-permute-done.6.rest_5_ = bf16[256,256]{1,0:T(8,128)(2,1)S(1)} collective-permute-done((bf16[256,256]{1,0:T(8,128)(2,1)S(1)}, bf16[256,256]{1,0:T(8,128)(2,1)S(1)}, u32[]{:S(2)}, u32[]{:S(2)}) %collective-permute-start.6) | collective-permute-done | bytes 131104 | tf_op jit(solution)/shard_map/ppermute | solution.py:300
  43.1 1.7 %shard_map.64 = (f32[8,8,256]{2,1,0:T(8,128)S(1)}, bf16[16,8,8,128]{3,2,1,0:T(8,128)(2,1)S(1)}) custom-call(s32[36]{0:T(128)S(1)} %concatenate.4.scalar_ref, bf16[8,2,9,8,128]{4,3,2,1,0:T(8,128)(2,1)S(1)} %maximum_bitcast_fusion.own_ref, bf16[8,2,9,8,128]{4,3,2,1,0:T(8,128)(2,1)S(1)} %collective-permute-done.1.other_ref, f32[8,8,256]{2,1,0:T(8,128)S(1)} %copy-done, ...), custom_call_target="tpu_custom_call" | custom-call | tf_op jit(solution)/shard_map/pallas_call | solution.py:326
  44.8 18.4 %all_to_all.15 = bf16[16,8,8,128]{3,2,1,0:T(8,128)(2,1)S(1)} all-to-all(bf16[16,8,8,128]{3,2,1,0:T(8,128)(2,1)S(1)} %get-tuple-element.29), channel_id=1, replica_groups=mesh['hist'=8,'x'=2,'c'=2] {'hist','x'}, dimensions={0} | all-to-all | bytes 524288 | tf_op jit(solution)/shard_map/all_to_all | solution.py:317
  63.2 1.5 %collective-permute-done.9.other_ref = bf16[8,2,8,8,128]{4,3,2,1,0:T(8,128)(2,1)S(1)} collective-permute-done((bf16[8,2,8,8,128]{4,3,2,1,0:T(8,128)(2,1)S(1)}, bf16[8,2,8,8,128]{4,3,2,1,0:T(8,128)(2,1)S(1)}, u32[]{:S(2)}, u32[]{:S(2)}) %collective-permute-start.9) | collective-permute-done | bytes 262176 | tf_op jit(solution)/shard_map/ppermute | solution.py:320
  64.7 1.8 %shard_map.65 = (f32[8,8,256]{2,1,0:T(8,128)S(1)}, bf16[16,8,8,128]{3,2,1,0:T(8,128)(2,1)S(1)}) custom-call(s32[36]{0:T(128)S(1)} %concatenate.4.scalar_ref, bf16[8,2,8,8,128]{4,3,2,1,0:T(8,128)(2,1)S(1)} %bitcast.18, bf16[8,2,8,8,128]{4,3,2,1,0:T(8,128)(2,1)S(1)} %collective-permute-done.9.other_ref, f32[8,8,256]{2,1,0:T(8,128)S(1)} %get-tuple-element.30.row_ref.rest_8_, ...), custom_call_target="tpu_custom_call" | custom-call | tf_op jit(solution)/shard_map/pallas_call | solution.py:326
  66.5 13.5 %all_to_all.16 = bf16[16,8,8,128]{3,2,1,0:T(8,128)(2,1)S(1)} all-to-all(bf16[16,8,8,128]{3,2,1,0:T(8,128)(2,1)S(1)} %get-tuple-element.32), channel_id=1, replica_groups=mesh['hist'=8,'x'=2,'c'=2] {'hist','x'}, dimensions={0} | all-to-all | bytes 524288 | tf_op jit(solution)/shard_map/all_to_all | solution.py:317
  80.0 1.5 %collective-permute-done.10.other_ref = bf16[8,2,8,8,128]{4,3,2,1,0:T(8,128)(2,1)S(1)} collective-permute-done((bf16[8,2,8,8,128]{4,3,2,1,0:T(8,128)(2,1)S(1)}, bf16[8,2,8,8,128]{4,3,2,1,0:T(8,128)(2,1)S(1)}, u32[]{:S(2)}, u32[]{:S(2)}) %collective-permute-start.10) | collective-permute-done | bytes 262176 | tf_op jit(solution)/shard_map/ppermute | solution.py:320
  81.6 2.2 %shard_map.66 = f32[8,8,256]{2,1,0:T(8,128)} custom-call(s32[36]{0:T(128)S(1)} %concatenate.4.scalar_ref, bf16[8,2,8,8,128]{4,3,2,1,0:T(8,128)(2,1)S(1)} %bitcast.16, bf16[8,2,8,8,128]{4,3,2,1,0:T(8,128)(2,1)S(1)} %collective-permute-done.10.other_ref, f32[8,8,256]{2,1,0:T(8,128)S(1)} %get-tuple-element.33.row_ref.rest_9_, ...), custom_call_target="tpu_custom_call" | custom-call | tf_op jit(solution)/shard_map/pallas_call | solution.py:326
  (23 shorter events, 0.7 us)
Async XLA Ops:
  1.7 14.8 %all-to-all-start = ((bf16[8,9,8,128]{3,2,1,0:T(8,128)(2,1)}), bf16[8,9,8,128]{3,2,1,0:T(8,128)(2,1)S(1)}, u32[]{:S(2)}, u32[]{:S(2)}) async-start(bf16[8,9,8,128]{3,2,1,0:T(8,128)(2,1)} %first.1), calls=%async_computation | async-start | bytes 294912 | tf_op jit(solution)/shard_map/all_to_all | solution.py:289
  16.5 8.2 %collective-permute-start = (bf16[1,8,9,8,128]{4,3,2,1,0:T(8,128)(2,1)S(1)}, bf16[1,8,9,8,128]{4,3,2,1,0:T(8,128)(2,1)S(1)}, u32[]{:S(2)}, u32[]{:S(2)}) collective-permute-start(bf16[1,8,9,8,128]{4,3,2,1,0:T(8,128)(2,1)S(1)} %bitcast.20), channel_id=1, source_target_pairs={{0,2},{2,0},{1,3},{3,1},{4,6},{6,4},{5,7},{7,5},{8,10},{10,8},{9,1... | collective-permute-start | bytes 442376 | tf_op jit(solution)/shard_map/ppermute | solution.py:242
  20.7 5.6 %collective-permute-start.2 = (bf16[256,256]{1,0:T(8,128)(2,1)S(1)}, bf16[256,256]{1,0:T(8,128)(2,1)S(1)}, u32[]{:S(2)}, u32[]{:S(2)}) collective-permute-start(bf16[256,256]{1,0:T(8,128)(2,1)S(1)} %get-tuple-element.21), channel_id=1, source_target_pairs={{0,4},{4,0},{8,12},{12,8},{16,20},{20,16},{24,28},{28,24},{1,5},{5... | collective-permute-start | bytes 393224 | tf_op jit(solution)/shard_map/ppermute | solution.py:300
  21.1 7.0 %collective-permute-start.3 = (bf16[256,256]{1,0:T(8,128)(2,1)S(1)}, bf16[256,256]{1,0:T(8,128)(2,1)S(1)}, u32[]{:S(2)}, u32[]{:S(2)}) collective-permute-start(bf16[256,256]{1,0:T(8,128)(2,1)S(1)} %get-tuple-element.22), channel_id=1, source_target_pairs={{0,8},{4,12},{8,0},{12,4},{16,24},{20,28},{24,16},{28,20},{1,9},{5... | collective-permute-start | bytes 393224 | tf_op jit(solution)/shard_map/ppermute | solution.py:300
  22.1 9.0 %collective-permute-start.4 = (bf16[256,256]{1,0:T(8,128)(2,1)S(1)}, bf16[256,256]{1,0:T(8,128)(2,1)S(1)}, u32[]{:S(2)}, u32[]{:S(2)}) collective-permute-start(bf16[256,256]{1,0:T(8,128)(2,1)S(1)} %get-tuple-element.23), channel_id=1, source_target_pairs={{0,12},{4,8},{8,4},{12,0},{16,28},{20,24},{24,20},{28,16},{1,13},{... | collective-permute-start | bytes 393224 | tf_op jit(solution)/shard_map/ppermute | solution.py:300
  24.2 16.5 %collective-permute-start.5 = (bf16[256,256]{1,0:T(8,128)(2,1)S(1)}, bf16[256,256]{1,0:T(8,128)(2,1)S(1)}, u32[]{:S(2)}, u32[]{:S(2)}) collective-permute-start(bf16[256,256]{1,0:T(8,128)(2,1)S(1)} %get-tuple-element.24), channel_id=1, source_target_pairs={{0,16},{4,20},{8,24},{12,28},{16,0},{20,4},{24,8},{28,12},{1,17},{... | collective-permute-start | bytes 393224 | tf_op jit(solution)/shard_map/ppermute | solution.py:300
  24.7 0.9 %copy-start.1 = (f32[3,2,64,64]{3,2,1,0:T(8,128)S(1)}, f32[3,2,64,64]{3,2,1,0:T(8,128)}, u32[]{:S(2)}) copy-start(f32[3,2,64,64]{3,2,1,0:T(8,128)} %pairs_ref.1) | copy-start | bytes 294916
  24.7 18.3 %collective-permute-start.1 = (bf16[8,2,9,8,128]{4,3,2,1,0:T(8,128)(2,1)S(1)}, bf16[8,2,9,8,128]{4,3,2,1,0:T(8,128)(2,1)S(1)}, u32[]{:S(2)}, u32[]{:S(2)}) collective-permute-start(bf16[8,2,9,8,128]{4,3,2,1,0:T(8,128)(2,1)S(1)} %maximum_bitcast_fusion.own_ref), channel_id=1, source_target_pairs={{0,1},{1,0},{2,3},{3,2},{4,5},{5,4},{6,7},{7,6},{8,9},{9,8},{10,11... | collective-permute-start | bytes 884744 | tf_op jit(solution)/shard_map/ppermute | solution.py:320
  25.6 17.4 %copy-start = (f32[8,8,256]{2,1,0:T(8,128)S(1)}, f32[8,8,256]{2,1,0:T(8,128)}, u32[]{:S(2)}) copy-start(f32[8,8,256]{2,1,0:T(8,128)} %row_ref.1) | copy-start | bytes 196612
  26.3 16.7 %collective-permute-start.6 = (bf16[256,256]{1,0:T(8,128)(2,1)S(1)}, bf16[256,256]{1,0:T(8,128)(2,1)S(1)}, u32[]{:S(2)}, u32[]{:S(2)}) collective-permute-start(bf16[256,256]{1,0:T(8,128)(2,1)S(1)} %get-tuple-element.25), channel_id=1, source_target_pairs={{0,20},{4,16},{8,28},{12,24},{16,4},{20,0},{24,12},{28,8},{1,21},{... | collective-permute-start | bytes 393224 | tf_op jit(solution)/shard_map/ppermute | solution.py:300
  28.1 15.0 %collective-permute-start.7 = (bf16[256,256]{1,0:T(8,128)(2,1)S(1)}, bf16[256,256]{1,0:T(8,128)(2,1)S(1)}, u32[]{:S(2)}, u32[]{:S(2)}) collective-permute-start(bf16[256,256]{1,0:T(8,128)(2,1)S(1)} %get-tuple-element.26), channel_id=1, source_target_pairs={{0,24},{4,28},{8,16},{12,20},{16,8},{20,12},{24,0},{28,4},{1,25},{... | collective-permute-start | bytes 393224 | tf_op jit(solution)/shard_map/ppermute | solution.py:300
  31.1 11.9 %collective-permute-start.8 = (bf16[256,256]{1,0:T(8,128)(2,1)S(1)}, bf16[256,256]{1,0:T(8,128)(2,1)S(1)}, u32[]{:S(2)}, u32[]{:S(2)}) collective-permute-start(bf16[256,256]{1,0:T(8,128)(2,1)S(1)} %get-tuple-element.27), channel_id=1, source_target_pairs={{0,28},{4,24},{8,20},{12,16},{16,12},{20,8},{24,4},{28,0},{1,29},{... | collective-permute-start | bytes 393224 | tf_op jit(solution)/shard_map/ppermute | solution.py:300
  33.4 9.6 %copy-start.2 = (f32[8,64]{1,0:T(8,128)S(1)}, f32[8,64]{1,0:T(8,128)}, u32[]{:S(2)}) copy-start(f32[8,64]{1,0:T(8,128)} %rest_11_.1) | copy-start | bytes 6148
  63.2 1.5 %collective-permute-start.9 = (bf16[8,2,8,8,128]{4,3,2,1,0:T(8,128)(2,1)S(1)}, bf16[8,2,8,8,128]{4,3,2,1,0:T(8,128)(2,1)S(1)}, u32[]{:S(2)}, u32[]{:S(2)}) collective-permute-start(bf16[8,2,8,8,128]{4,3,2,1,0:T(8,128)(2,1)S(1)} %bitcast.17), channel_id=1, source_target_pairs={{0,1},{1,0},{2,3},{3,2},{4,5},{5,4},{6,7},{7,6},{8,9},{9,8},{10,11... | collective-permute-start | bytes 786440 | tf_op jit(solution)/shard_map/ppermute | solution.py:320
  80.0 1.5 %collective-permute-start.10 = (bf16[8,2,8,8,128]{4,3,2,1,0:T(8,128)(2,1)S(1)}, bf16[8,2,8,8,128]{4,3,2,1,0:T(8,128)(2,1)S(1)}, u32[]{:S(2)}, u32[]{:S(2)}) collective-permute-start(bf16[8,2,8,8,128]{4,3,2,1,0:T(8,128)(2,1)S(1)} %bitcast.15), channel_id=1, source_target_pairs={{0,1},{1,0},{2,3},{3,2},{4,5},{5,4},{6,7},{7,6},{8,9},{9,8},{10,11... | collective-permute-start | bytes 786440 | tf_op jit(solution)/shard_map/ppermute | solution.py:320

commit v5 on v3

--- a/solution.py
+++ b/solution.py
@@ -9,7 +9,6 @@
 
 
 step_width = 0.05
-highest = lax.Precision.HIGHEST
 bf16 = jnp.bfloat16
 f32 = jnp.float32
 vmem = pl.BlockSpec(memory_space=pltpu.VMEM)
@@ -43,7 +42,8 @@
         wide_ref[chunks[c], :] = hist_ref[chunks[c], :].astype(f32)
         columns = slice(c * 128, (c + 1) * 128)
         for group in range(groups):
-            turned = wide_ref[pl.ds(c * rows + group, 128, stride=groups), :].T
+            tile = wide_ref[pl.ds(c * rows + group, 128, stride=groups), :]
+            turned = tile.astype(bf16).T.astype(f32)
             for peer in range(len(out_refs)):
                 turned_ref[group % 2, peer] = turned[peer * width : (peer + 1) * width]
             for offset, out_ref in enumerate(out_refs):
@@ -109,9 +109,12 @@
 def build_kernel(pairs_ref, *out_refs):
     for w, out_ref in enumerate(out_refs):
         real, imag = pairs_ref[w, 0], pairs_ref[w, 1]
-        size = real.shape[0]
-        out_ref[:size, :] = jnp.concatenate([real, -imag], axis=1)
-        out_ref[size:, :] = jnp.concatenate([imag, real], axis=1)
+        rows = [jnp.concatenate([real, -imag], axis=1), jnp.concatenate([imag, real], axis=1)]
+        turned = jnp.concatenate(rows, axis=0).T
+        high = turned.astype(bf16)
+        size = turned.shape[0]
+        out_ref[:, :size] = high
+        out_ref[:, size:] = (turned - high.astype(f32)).astype(bf16)
 
 
 def energy_at(time, slab, place, core, own_ref, other_ref):
@@ -123,13 +126,6 @@
         jnp.where(same, own_ref[peer, far, inner], other_ref[peer, far, inner])
         for peer in range(own_ref.shape[0])
     ]
-
-
-def choose(time, alive, slab, place, core, own_ref, other_ref, chosen_ref, slot):
-    own_rows = own_ref.shape[3]
-    for peer, part in enumerate(energy_at(time, slab, place, core, own_ref, other_ref)):
-        part = jnp.where(alive, part, jnp.zeros_like(part))
-        chosen_ref[slot, peer * own_rows : (peer + 1) * own_rows, :] = part
 
 
 def signs(lanes):
@@ -168,13 +164,12 @@
             integral += jnp.dot(low, column, preferred_element_type=f32)
         row = row_ref[:, :, m * lanes : (m + 1) * lanes].reshape(own_rows * slab, lanes)
         moved.append(row + step_width * integral)
-    moved = lax.dot_general(
-        jnp.concatenate(moved, axis=0),
-        inverse_ref[...],
-        (((1,), (1,)), ((), ())),
-        precision=highest,
-        preferred_element_type=f32,
-    )
+    moved = jnp.concatenate(moved, axis=0)
+    high = moved.astype(bf16)
+    low = (moved - high.astype(f32)).astype(bf16)
+    both = jnp.dot(high, inverse_ref[...], preferred_element_type=f32)
+    rest = jnp.dot(low, inverse_ref[:, :lanes], preferred_element_type=f32)
+    moved = both[:, :lanes] + (both[:, lanes:] + rest)
     for m in range(2):
         out_ref[:, :, m * lanes : (m + 1) * lanes] = moved[
             m * own_rows * slab : (m + 1) * own_rows * slab
@@ -191,23 +186,22 @@
         send_ref = energy_ref = None
     else:
         send_ref, chosen_ref, sum_ref, energy_ref = rest
-    slab = row_ref.shape[1]
+    own_rows, slab = row_ref.shape[:2]
     slots, orbitals, lanes = chosen_ref.shape
     block = slots // peers
-    anchor, home, place, core = [scalar_ref[slots + i] for i in range(4)]
+    anchor, place, core = [scalar_ref[slots + i] for i in (0, 2, 3)]
     place = place if relative else 0
 
     def select(source, slot):
-        time = scalar_ref[(source ^ home) * block + slot]
+        time = scalar_ref[source * block + slot]
         alive = time <= anchor
-        to = source * block + slot
-        choose(time, alive, slab, place, core, own_ref, other_ref, chosen_ref, to)
-
-    if slots <= 32:
-        for source in range(peers):
-            for slot in range(block):
-                select(source, slot)
-    else:
+        parts = energy_at(time, slab, place, core, own_ref, other_ref)
+        for peer, part in enumerate(parts):
+            chosen_ref[
+                source * block + slot, peer * own_rows : (peer + 1) * own_rows, :
+            ] = jnp.where(alive, part, jnp.zeros_like(part))
+
+    if slots > 32:
 
         @pl.loop(0, peers)
         def _(source):
@@ -216,6 +210,9 @@
 
     total = None
     for peer in range(peers):
+        if slots <= 32:
+            for slot in range(block):
+                select(peer, slot)
         part = jnp.dot(
             hist_refs[peer][...],
             chosen_ref[peer * block : (peer + 1) * block].reshape(block * orbitals, lanes),
@@ -225,7 +222,9 @@
     sum_ref[...] = combined(total)
     columns = []
     for past in range(n_past):
-        choose(anchor + 1 + past, True, slab, place, core, own_ref, other_ref, chosen_ref, past)
+        parts = energy_at(anchor + 1 + past, slab, place, core, own_ref, other_ref)
+        for peer, part in enumerate(parts):
+            chosen_ref[past, peer * own_rows : (peer + 1) * own_rows, :] = part
         columns.append(chosen_ref[past])
     advance(sum_ref, row_ref, past_refs, columns, inverse_ref, out_ref)
     if not last:
@@ -287,7 +286,8 @@
     )(remote(row_now), remote(coupling), remote(history_time))
     own = lax.all_to_all(sent, "hist", split_axis=0, concat_axis=0, tiled=True)
     times = own[:, slab, 0, :slots_dev].astype(jnp.int32).reshape(peers * slots_dev)
-    scalars = jnp.concatenate([times, start_step, place])
+    nearest = jnp.take(times.reshape(peers, slots_dev), jnp.arange(peers) ^ place[0], axis=0)
+    scalars = jnp.concatenate([nearest.reshape(-1), start_step, place])
     scalars = pltpu.with_memory_space_constraint(scalars, pltpu.SMEM)
     own = spread(own, "x").swapaxes(0, 1)
     moved = [packed[0]]
@@ -296,7 +296,7 @@
         moved.append(lax.ppermute(packed[offset], "hist", ring))
     inverse = pl.pallas_call(
         build_kernel,
-        out_shape=[pltpu.VMEM((2 * orbitals, 2 * orbitals), f32)] * steps,
+        out_shape=[pltpu.VMEM((2 * orbitals, 4 * orbitals), bf16)] * steps,
         in_specs=[vmem],
         out_specs=[vmem] * steps,
         compiler_params=params,

time: 88.2 us -> 81.9 us (0.929)
  blocking collectives: 46 us -> 32.3 us
  starting transfers between devices: 13.6 us -> 20.3 us
    all_to_all x1 -> x0, blocking collectives: 14.6 us -> none  [body(): own = lax.all_to_all(sent, 'hist', split_axis=0, concat_axis=0, tiled=True)]
    all_to_all x0 -> x1, starting transfers between devices: none -> 7.32 us  [body(): own = lax.all_to_all(sent, 'hist', split_axis=0, concat_axis=0, tiled=True)]
    ppermute x1, waiting for transfers between devices: 3.65 us -> 2.74 us  [spread(): other = lax.ppermute(gathered, axis, ring)]
    all_to_all x2, blocking collectives: 31.4 us -> 32.3 us  [body(): lax.all_to_all(sent, ('hist', 'x'), split_axis=0, concat_axis=0, tiled=True)]
  transfers between devices with their start and end apart: 11 -> 12, of which waited for: 8 -> 4; matrix products, arithmetic and copies ran while one was open for 0% -> 1% of each run, Pallas kernels for 3% -> 3%
where the time goes in v5:
time: 81.9 us; the launch traced here: 81.5 us
  blocking collectives  32.3 us (39%)
  starting transfers between devices  20.3 us (25%)
  waiting for transfers between devices  17.4 us (21%)
  Pallas kernels  9.86 us (12%)
    all_to_all x2, blocking collectives, body(): lax.all_to_all(sent, ('hist', 'x'), split_axis=0, concat_axis=0, tiled=True)  32.3 us
    ppermute x7, waiting for transfers between devices, body(): moved.append(lax.ppermute(packed[offset], 'hist', ring))  11.5 us
    ppermute x7, starting transfers between devices, body(): moved.append(lax.ppermute(packed[offset], 'hist', ring))  11.4 us
    all_to_all x1, starting transfers between devices, body(): own = lax.all_to_all(sent, 'hist', split_axis=0, concat_axis=0, tiled=True)  7.32 us
    pallas_call x3, Pallas kernels, body(): pl.pallas_call(functools.partial(step_kernel, peers, len(past), w == 0, l...  5.33 us
    ppermute x3, waiting for transfers between devices, body(): other = lax.ppermute(own, 'c', swap)  3.07 us
    ppermute x1, waiting for transfers between devices, spread(): other = lax.ppermute(gathered, axis, ring)  2.74 us
    pallas_call x1, Pallas kernels, body(): pl.pallas_call(functools.partial(pack_kernel, groups), out_shape=[pltpu.V...  2.59 us
  transfers between devices with their start and end apart: 12, of which 4 were waited for; matrix products, arithmetic and copies ran while one was open for 1% of the time, Pallas kernels for 3%

profile of v5, /device:TPU:0, one launch (start us, length us, event | category | flops | bytes accessed | tf_op | source)
XLA Modules:
  0.0 81.5 jit_solution(1508149672296744113)
XLA Ops:
  0.0 1.7 %first.1 = bf16[8,9,8,128]{3,2,1,0:T(8,128)(2,1)} custom-call(f32[8,8,256]{2,1,0:T(8,128)} %row_ref.1, f32[8,64]{1,0:T(8,128)} %rest_11_.1, s32[4]{0:T(128)} %time_hbm.1), custom_call_target="tpu_custom_call" | custom-call | tf_op jit(solution)/shard_map/first/pallas_call | solution.py:272
  1.7 7.3 %all-to-all-start = ((bf16[8,9,8,128]{3,2,1,0:T(8,128)(2,1)}), bf16[8,9,8,128]{3,2,1,0:T(8,128)(2,1)S(1)}, u32[]{:S(2)}, u32[]{:S(2)}) async-start(bf16[8,9,8,128]{3,2,1,0:T(8,128)(2,1)} %first.1), calls=%async_computation | async-start | bytes 294912 | tf_op jit(solution)/shard_map/all_to_all | solution.py:287
  9.1 0.1 pad_add_fusion.place_ref
  9.1 2.6 %pack.1 = (bf16[256,256]{1,0:T(8,128)(2,1)S(1)}, bf16[256,256]{1,0:T(8,128)(2,1)S(1)}, bf16[256,256]{1,0:T(8,128)(2,1)S(1)}, bf16[256,256]{1,0:T(8,128)(2,1)S(1)...) custom-call(s32[3]{0:T(128)S(1)} %pad_add_fusion.place_ref, ...), custom_call_target="tpu_custom_call" | custom-call | tf_op jit(solution)/shard_map/pack/pallas_call | solution.py:258
  11.7 2.1 %collective-permute-start.2 = (bf16[256,256]{1,0:T(8,128)(2,1)S(1)}, bf16[256,256]{1,0:T(8,128)(2,1)S(1)}, u32[]{:S(2)}, u32[]{:S(2)}) collective-permute-start(bf16[256,256]{1,0:T(8,128)(2,1)S(1)} %get-tuple-element.21), channel_id=1, source_target_pairs={{0,4},{4,0},{8,12},{12,8},{16,20},{20,16},{24,28},{28,24},{1,5},{5... | collective-permute-start | bytes 393224 | tf_op jit(solution)/shard_map/ppermute | solution.py:296
  13.8 1.5 %collective-permute-start.3 = (bf16[256,256]{1,0:T(8,128)(2,1)S(1)}, bf16[256,256]{1,0:T(8,128)(2,1)S(1)}, u32[]{:S(2)}, u32[]{:S(2)}) collective-permute-start(bf16[256,256]{1,0:T(8,128)(2,1)S(1)} %get-tuple-element.22), channel_id=1, source_target_pairs={{0,8},{4,12},{8,0},{12,4},{16,24},{20,28},{24,16},{28,20},{1,9},{5... | collective-permute-start | bytes 393224 | tf_op jit(solution)/shard_map/ppermute | solution.py:296
  15.4 2.9 %collective-permute-start.5 = (bf16[256,256]{1,0:T(8,128)(2,1)S(1)}, bf16[256,256]{1,0:T(8,128)(2,1)S(1)}, u32[]{:S(2)}, u32[]{:S(2)}) collective-permute-start(bf16[256,256]{1,0:T(8,128)(2,1)S(1)} %get-tuple-element.24), channel_id=1, source_target_pairs={{0,16},{4,20},{8,24},{12,28},{16,0},{20,4},{24,8},{28,12},{1,17},{... | collective-permute-start | bytes 393224 | tf_op jit(solution)/shard_map/ppermute | solution.py:296
  18.2 1.6 %collective-permute-start = (bf16[1,8,9,8,128]{4,3,2,1,0:T(8,128)(2,1)S(1)}, bf16[1,8,9,8,128]{4,3,2,1,0:T(8,128)(2,1)S(1)}, u32[]{:S(2)}, u32[]{:S(2)}) collective-permute-start(bf16[1,8,9,8,128]{4,3,2,1,0:T(8,128)(2,1)S(1)} %bitcast.23), channel_id=1, source_target_pairs={{0,2},{2,0},{1,3},{3,1},{4,6},{6,4},{5,7},{7,5},{8,10},{10,8},{9,1... | collective-permute-start | bytes 442376 | tf_op jit(solution)/shard_map/ppermute | solution.py:240
  20.5 0.2 build.1
  20.7 2.7 %collective-permute-done = bf16[1,8,9,8,128]{4,3,2,1,0:T(8,128)(2,1)S(1)} collective-permute-done((bf16[1,8,9,8,128]{4,3,2,1,0:T(8,128)(2,1)S(1)}, bf16[1,8,9,8,128]{4,3,2,1,0:T(8,128)(2,1)S(1)}, u32[]{:S(2)}, u32[]{:S(2)}) %collective-permute-start) | collective-permute-done | bytes 147488 | tf_op jit(solution)/shard_map/ppermute | solution.py:240
  23.5 0.1 collective-permute-start.1
  23.6 0.6 gather_fusion
  24.1 1.5 %collective-permute-start.6 = (bf16[256,256]{1,0:T(8,128)(2,1)S(1)}, bf16[256,256]{1,0:T(8,128)(2,1)S(1)}, u32[]{:S(2)}, u32[]{:S(2)}) collective-permute-start(bf16[256,256]{1,0:T(8,128)(2,1)S(1)} %get-tuple-element.25), channel_id=1, source_target_pairs={{0,20},{4,16},{8,28},{12,24},{16,4},{20,0},{24,12},{28,8},{1,21},{... | collective-permute-start | bytes 393224 | tf_op jit(solution)/shard_map/ppermute | solution.py:296
  25.7 3.3 %collective-permute-start.7 = (bf16[256,256]{1,0:T(8,128)(2,1)S(1)}, bf16[256,256]{1,0:T(8,128)(2,1)S(1)}, u32[]{:S(2)}, u32[]{:S(2)}) collective-permute-start(bf16[256,256]{1,0:T(8,128)(2,1)S(1)} %get-tuple-element.26), channel_id=1, source_target_pairs={{0,24},{4,28},{8,16},{12,20},{16,8},{20,12},{24,0},{28,4},{1,25},{... | collective-permute-start | bytes 393224 | tf_op jit(solution)/shard_map/ppermute | solution.py:296
  29.1 0.1 select_n.27
  29.2 0.1 concatenate.4.scalar_ref
  29.3 11.5 %collective-permute-done.6.rest_5_ = bf16[256,256]{1,0:T(8,128)(2,1)S(1)} collective-permute-done((bf16[256,256]{1,0:T(8,128)(2,1)S(1)}, bf16[256,256]{1,0:T(8,128)(2,1)S(1)}, u32[]{:S(2)}, u32[]{:S(2)}) %collective-permute-start.6) | collective-permute-done | bytes 131104 | tf_op jit(solution)/shard_map/ppermute | solution.py:296
  40.8 1.6 %shard_map.64 = (f32[8,8,256]{2,1,0:T(8,128)S(1)}, bf16[16,8,8,128]{3,2,1,0:T(8,128)(2,1)S(1)}) custom-call(s32[36]{0:T(128)S(1)} %concatenate.4.scalar_ref, bf16[8,2,9,8,128]{4,3,2,1,0:T(8,128)(2,1)S(1)} %maximum_bitcast_fusion.own_ref, bf16[8,2,9,8,128]{4,3,2,1,0:T(8,128)(2,1)S(1)} %collective-permute-done.1.other_ref, f32[8,8,256]{2,1,0:T(8,128)S(1)} %copy-done, ...), custom_call_target="tpu_custom_call" | custom-call | tf_op jit(solution)/shard_map/pallas_call | solution.py:322
  42.5 18.8 %all_to_all.15 = bf16[16,8,8,128]{3,2,1,0:T(8,128)(2,1)S(1)} all-to-all(bf16[16,8,8,128]{3,2,1,0:T(8,128)(2,1)S(1)} %get-tuple-element.29), channel_id=1, replica_groups=mesh['hist'=8,'x'=2,'c'=2] {'hist','x'}, dimensions={0} | all-to-all | bytes 524288 | tf_op jit(solution)/shard_map/all_to_all | solution.py:313
  61.2 1.5 %collective-permute-done.9.other_ref = bf16[8,2,8,8,128]{4,3,2,1,0:T(8,128)(2,1)S(1)} collective-permute-done((bf16[8,2,8,8,128]{4,3,2,1,0:T(8,128)(2,1)S(1)}, bf16[8,2,8,8,128]{4,3,2,1,0:T(8,128)(2,1)S(1)}, u32[]{:S(2)}, u32[]{:S(2)}) %collective-permute-start.9) | collective-permute-done | bytes 262176 | tf_op jit(solution)/shard_map/ppermute | solution.py:316
  62.8 1.6 %shard_map.65 = (f32[8,8,256]{2,1,0:T(8,128)S(1)}, bf16[16,8,8,128]{3,2,1,0:T(8,128)(2,1)S(1)}) custom-call(s32[36]{0:T(128)S(1)} %concatenate.4.scalar_ref, bf16[8,2,8,8,128]{4,3,2,1,0:T(8,128)(2,1)S(1)} %bitcast.21, bf16[8,2,8,8,128]{4,3,2,1,0:T(8,128)(2,1)S(1)} %collective-permute-done.9.other_ref, f32[8,8,256]{2,1,0:T(8,128)S(1)} %get-tuple-element.30.row_ref.rest_8_, ...), custom_call_target="tpu_custom_call" | custom-call | tf_op jit(solution)/shard_map/pallas_call | solution.py:322
  64.4 13.5 %all_to_all.16 = bf16[16,8,8,128]{3,2,1,0:T(8,128)(2,1)S(1)} all-to-all(bf16[16,8,8,128]{3,2,1,0:T(8,128)(2,1)S(1)} %get-tuple-element.32), channel_id=1, replica_groups=mesh['hist'=8,'x'=2,'c'=2] {'hist','x'}, dimensions={0} | all-to-all | bytes 524288 | tf_op jit(solution)/shard_map/all_to_all | solution.py:313
  77.9 1.5 %collective-permute-done.10.other_ref = bf16[8,2,8,8,128]{4,3,2,1,0:T(8,128)(2,1)S(1)} collective-permute-done((bf16[8,2,8,8,128]{4,3,2,1,0:T(8,128)(2,1)S(1)}, bf16[8,2,8,8,128]{4,3,2,1,0:T(8,128)(2,1)S(1)}, u32[]{:S(2)}, u32[]{:S(2)}) %collective-permute-start.10) | collective-permute-done | bytes 262176 | tf_op jit(solution)/shard_map/ppermute | solution.py:316
  79.5 2.1 %shard_map.66 = f32[8,8,256]{2,1,0:T(8,128)} custom-call(s32[36]{0:T(128)S(1)} %concatenate.4.scalar_ref, bf16[8,2,8,8,128]{4,3,2,1,0:T(8,128)(2,1)S(1)} %bitcast.19, bf16[8,2,8,8,128]{4,3,2,1,0:T(8,128)(2,1)S(1)} %collective-permute-done.10.other_ref, f32[8,8,256]{2,1,0:T(8,128)S(1)} %get-tuple-element.33.row_ref.rest_9_, ...), custom_call_target="tpu_custom_call" | custom-call | tf_op jit(solution)/shard_map/pallas_call | solution.py:322
  (24 shorter events, 0.3 us)
Async XLA Ops:
  1.7 16.5 %all-to-all-start = ((bf16[8,9,8,128]{3,2,1,0:T(8,128)(2,1)}), bf16[8,9,8,128]{3,2,1,0:T(8,128)(2,1)S(1)}, u32[]{:S(2)}, u32[]{:S(2)}) async-start(bf16[8,9,8,128]{3,2,1,0:T(8,128)(2,1)} %first.1), calls=%async_computation | async-start | bytes 294912 | tf_op jit(solution)/shard_map/all_to_all | solution.py:287
  9.1 11.3 %copy-start.1 = (f32[3,2,64,64]{3,2,1,0:T(8,128)S(1)}, f32[3,2,64,64]{3,2,1,0:T(8,128)}, u32[]{:S(2)}) copy-start(f32[3,2,64,64]{3,2,1,0:T(8,128)} %pairs_ref.1) | copy-start | bytes 294916
  11.7 12.4 %collective-permute-start.2 = (bf16[256,256]{1,0:T(8,128)(2,1)S(1)}, bf16[256,256]{1,0:T(8,128)(2,1)S(1)}, u32[]{:S(2)}, u32[]{:S(2)}) collective-permute-start(bf16[256,256]{1,0:T(8,128)(2,1)S(1)} %get-tuple-element.21), channel_id=1, source_target_pairs={{0,4},{4,0},{8,12},{12,8},{16,20},{20,16},{24,28},{28,24},{1,5},{5... | collective-permute-start | bytes 393224 | tf_op jit(solution)/shard_map/ppermute | solution.py:296
  13.8 11.8 %collective-permute-start.3 = (bf16[256,256]{1,0:T(8,128)(2,1)S(1)}, bf16[256,256]{1,0:T(8,128)(2,1)S(1)}, u32[]{:S(2)}, u32[]{:S(2)}) collective-permute-start(bf16[256,256]{1,0:T(8,128)(2,1)S(1)} %get-tuple-element.22), channel_id=1, source_target_pairs={{0,8},{4,12},{8,0},{12,4},{16,24},{20,28},{24,16},{28,20},{1,9},{5... | collective-permute-start | bytes 393224 | tf_op jit(solution)/shard_map/ppermute | solution.py:296
  15.3 13.7 %collective-permute-start.4 = (bf16[256,256]{1,0:T(8,128)(2,1)S(1)}, bf16[256,256]{1,0:T(8,128)(2,1)S(1)}, u32[]{:S(2)}, u32[]{:S(2)}) collective-permute-start(bf16[256,256]{1,0:T(8,128)(2,1)S(1)} %get-tuple-element.23), channel_id=1, source_target_pairs={{0,12},{4,8},{8,4},{12,0},{16,28},{20,24},{24,20},{28,16},{1,13},{... | collective-permute-start | bytes 393224 | tf_op jit(solution)/shard_map/ppermute | solution.py:296
  15.4 13.9 %collective-permute-start.5 = (bf16[256,256]{1,0:T(8,128)(2,1)S(1)}, bf16[256,256]{1,0:T(8,128)(2,1)S(1)}, u32[]{:S(2)}, u32[]{:S(2)}) collective-permute-start(bf16[256,256]{1,0:T(8,128)(2,1)S(1)} %get-tuple-element.24), channel_id=1, source_target_pairs={{0,16},{4,20},{8,24},{12,28},{16,0},{20,4},{24,8},{28,12},{1,17},{... | collective-permute-start | bytes 393224 | tf_op jit(solution)/shard_map/ppermute | solution.py:296
  18.2 5.2 %collective-permute-start = (bf16[1,8,9,8,128]{4,3,2,1,0:T(8,128)(2,1)S(1)}, bf16[1,8,9,8,128]{4,3,2,1,0:T(8,128)(2,1)S(1)}, u32[]{:S(2)}, u32[]{:S(2)}) collective-permute-start(bf16[1,8,9,8,128]{4,3,2,1,0:T(8,128)(2,1)S(1)} %bitcast.23), channel_id=1, source_target_pairs={{0,2},{2,0},{1,3},{3,1},{4,6},{6,4},{5,7},{7,5},{8,10},{10,8},{9,1... | collective-permute-start | bytes 442376 | tf_op jit(solution)/shard_map/ppermute | solution.py:240
  23.5 17.4 %copy-start = (f32[8,8,256]{2,1,0:T(8,128)S(1)}, f32[8,8,256]{2,1,0:T(8,128)}, u32[]{:S(2)}) copy-start(f32[8,8,256]{2,1,0:T(8,128)} %row_ref.1) | copy-start | bytes 196612
  23.5 17.3 %collective-permute-start.1 = (bf16[8,2,9,8,128]{4,3,2,1,0:T(8,128)(2,1)S(1)}, bf16[8,2,9,8,128]{4,3,2,1,0:T(8,128)(2,1)S(1)}, u32[]{:S(2)}, u32[]{:S(2)}) collective-permute-start(bf16[8,2,9,8,128]{4,3,2,1,0:T(8,128)(2,1)S(1)} %maximum_bitcast_fusion.own_ref), channel_id=1, source_target_pairs={{0,1},{1,0},{2,3},{3,2},{4,5},{5,4},{6,7},{7,6},{8,9},{9,8},{10,11... | collective-permute-start | bytes 884744 | tf_op jit(solution)/shard_map/ppermute | solution.py:316
  24.1 16.7 %collective-permute-start.6 = (bf16[256,256]{1,0:T(8,128)(2,1)S(1)}, bf16[256,256]{1,0:T(8,128)(2,1)S(1)}, u32[]{:S(2)}, u32[]{:S(2)}) collective-permute-start(bf16[256,256]{1,0:T(8,128)(2,1)S(1)} %get-tuple-element.25), channel_id=1, source_target_pairs={{0,20},{4,16},{8,28},{12,24},{16,4},{20,0},{24,12},{28,8},{1,21},{... | collective-permute-start | bytes 393224 | tf_op jit(solution)/shard_map/ppermute | solution.py:296
  25.7 15.2 %collective-permute-start.7 = (bf16[256,256]{1,0:T(8,128)(2,1)S(1)}, bf16[256,256]{1,0:T(8,128)(2,1)S(1)}, u32[]{:S(2)}, u32[]{:S(2)}) collective-permute-start(bf16[256,256]{1,0:T(8,128)(2,1)S(1)} %get-tuple-element.26), channel_id=1, source_target_pairs={{0,24},{4,28},{8,16},{12,20},{16,8},{20,12},{24,0},{28,4},{1,25},{... | collective-permute-start | bytes 393224 | tf_op jit(solution)/shard_map/ppermute | solution.py:296
  29.0 11.8 %collective-permute-start.8 = (bf16[256,256]{1,0:T(8,128)(2,1)S(1)}, bf16[256,256]{1,0:T(8,128)(2,1)S(1)}, u32[]{:S(2)}, u32[]{:S(2)}) collective-permute-start(bf16[256,256]{1,0:T(8,128)(2,1)S(1)} %get-tuple-element.27), channel_id=1, source_target_pairs={{0,28},{4,24},{8,20},{12,16},{16,12},{20,8},{24,4},{28,0},{1,29},{... | collective-permute-start | bytes 393224 | tf_op jit(solution)/shard_map/ppermute | solution.py:296
  29.2 11.6 %copy-start.2 = (f32[8,64]{1,0:T(8,128)S(1)}, f32[8,64]{1,0:T(8,128)}, u32[]{:S(2)}) copy-start(f32[8,64]{1,0:T(8,128)} %rest_11_.1) | copy-start | bytes 6148
  61.2 1.5 %collective-permute-start.9 = (bf16[8,2,8,8,128]{4,3,2,1,0:T(8,128)(2,1)S(1)}, bf16[8,2,8,8,128]{4,3,2,1,0:T(8,128)(2,1)S(1)}, u32[]{:S(2)}, u32[]{:S(2)}) collective-permute-start(bf16[8,2,8,8,128]{4,3,2,1,0:T(8,128)(2,1)S(1)} %bitcast.20), channel_id=1, source_target_pairs={{0,1},{1,0},{2,3},{3,2},{4,5},{5,4},{6,7},{7,6},{8,9},{9,8},{10,11... | collective-permute-start | bytes 786440 | tf_op jit(solution)/shard_map/ppermute | solution.py:316
  77.9 1.5 %collective-permute-start.10 = (bf16[8,2,8,8,128]{4,3,2,1,0:T(8,128)(2,1)S(1)}, bf16[8,2,8,8,128]{4,3,2,1,0:T(8,128)(2,1)S(1)}, u32[]{:S(2)}, u32[]{:S(2)}) collective-permute-start(bf16[8,2,8,8,128]{4,3,2,1,0:T(8,128)(2,1)S(1)} %bitcast.18), channel_id=1, source_target_pairs={{0,1},{1,0},{2,3},{3,2},{4,5},{5,4},{6,7},{7,6},{8,9},{9,8},{10,11... | collective-permute-start | bytes 786440 | tf_op jit(solution)/shard_map/ppermute | solution.py:316
